TPU v7x, 256 devices: a whole 4x4x8 slice. The times are simulated.
256 devices in a mesh: row: 128 (over y, z, x), head: 2 (over core).
Axes of the slice: x: 4, y: 4, z: 8, core: 2. Of those that a mesh axis runs over, the one named last changes fastest.
Arguments:
- query_single: bfloat16 [128, 384], P('row'), may hold values from -6 to 6
- key_single: bfloat16 [8192, 384], P('row'), may hold values from -6 to 6
- pair: bfloat16 [128, 8192, 128], P('row'), may hold values from -6 to 32
- query_frames: float32 [12, 128], P(None, 'row'), may hold values from -2.5 to 2.5, as said below
- key_frames: float32 [12, 8192], P(None, 'row'), may hold values from -2.5 to 2.5, as said below
- w_query: bfloat16 [384, 96], P(None, 'head'), may hold values from -0.3125 to 0.3125
- w_key: bfloat16 [384, 96], P(None, 'head'), may hold values from -0.3125 to 0.3125
- w_value: bfloat16 [384, 96], P(None, 'head'), may hold values from -0.3125 to 0.3125
- w_query_points: bfloat16 [384, 72], P(None, 'head'), may hold values from -0.3125 to 0.3125
- w_key_points: bfloat16 [384, 72], P(None, 'head'), may hold values from -0.3125 to 0.3125
- w_value_points: bfloat16 [384, 144], P(None, 'head'), may hold values from -0.3125 to 0.3125
- head_weight: float32 [6], P('head'), may hold values from -2.5 to 0.5
- bias_weight: bfloat16 [6, 128], P('head'), as said below
- w_out: bfloat16 [1056, 384], P('head'), may hold values from -0.1875 to 0.1875
- d_out: bfloat16 [128, 384], P('row'), may hold values from -24 to 24
Outputs:
- output: bfloat16 [128, 384], P('row')
- grad_query: float32 [128, 384], P('row')
- grad_keys: float32 [8192, 384], P('row')
Inputs may be any that keep to these rules, and one draw needn't show every extreme that they name: `bias_weight`: entries within -2.5 and 2.5 over the square root of 128. `query_frames`: rows 0 to 8 of each column form a rotation matrix. `key_frames`: rows 0 to 8 of each column form a rotation matrix.
All inputs are finite; a program needn't handle non-finite values.
Results may differ from a plain program's by a relative error of at most 0.012.
The roundings to bfloat16 on the way count: a program that leaves them out, or rounds other values in their place, can miss the bound.
Values may be sent and summed in bfloat16 or wider, within the bound.
A program may use at most 64 MiB of HBM per device.

v0:
```python
import math

import jax
import jax.numpy as jnp
from jax import lax
from jax.sharding import PartitionSpec as P

C = 16
PQ = 4
PV = 8


LOGIT_SCALE = math.sqrt(1.0 / 3.0)


def point_scale(points):
    return math.sqrt(2.0 / (9.0 * points))


def product(form, former, latter):
    return jnp.einsum(form, former, latter, preferred_element_type=jnp.float32)


def frame_parts(frames):
    columns = frames.shape[1]
    return (frames[:9].reshape(3, 3, columns), frames[9:12])


def rotate(vectors, rotation):
    return jnp.einsum("xyn,nhpy->nhpx", rotation, vectors, precision=lax.Precision.HIGHEST)


def unrotate(vectors, rotation):
    return jnp.einsum("xyn,nhpx->nhpy", rotation, vectors, precision=lax.Precision.HIGHEST)


def split_columns(packed, extents, axis_index):
    pieces = []
    cursor = 0
    for extent in extents:
        pieces.append(lax.slice_in_dim(packed, cursor, cursor + extent, axis=axis_index))
        cursor = cursor + extent
    return pieces


def key_side(key_single, key_frames, w_key, w_value, w_key_points, w_value_points, head_count):
    rows_k = key_single.shape[0]
    rotation, offset = frame_parts(key_frames)
    offset_rows = jnp.transpose(offset)[:, None, None, :]
    keys_b = jnp.dot(key_single, w_key, preferred_element_type=jnp.float32).astype(jnp.bfloat16)
    values_b = jnp.dot(key_single, w_value, preferred_element_type=jnp.float32).astype(jnp.bfloat16)
    local_k = jnp.dot(key_single, w_key_points, preferred_element_type=jnp.float32).reshape(
        rows_k, head_count, PQ, 3
    )
    key_pts = (rotate(local_k, rotation) + offset_rows).astype(jnp.bfloat16).reshape(rows_k, -1)
    local_v = jnp.dot(key_single, w_value_points, preferred_element_type=jnp.float32).reshape(
        rows_k, head_count, PV, 3
    )
    value_pts = (rotate(local_v, rotation) + offset_rows).astype(jnp.bfloat16).reshape(rows_k, -1)
    return (keys_b, values_b, key_pts, value_pts)


def query_pass(
    query_single,
    pair,
    query_frames,
    w_query,
    w_query_points,
    head_weight,
    bias_weight,
    w_out,
    d_out,
    keys_all,
    values_all,
    kp_all,
    vp_all,
):
    rows_q = query_single.shape[0]
    head_count = head_weight.shape[0]
    rotation, offset = frame_parts(query_frames)
    offset_rows = jnp.transpose(offset)[:, None, None, :]
    point_gain = (jax.nn.softplus(head_weight) * point_scale(PQ))[None, :, None]
    query_b = (
        jnp.dot(query_single, w_query, preferred_element_type=jnp.float32)
        .astype(jnp.bfloat16)
        .reshape(rows_q, head_count, C)
    )
    local_q = jnp.dot(query_single, w_query_points, preferred_element_type=jnp.float32).reshape(
        rows_q, head_count, PQ, 3
    )
    query_pts = (
        (rotate(local_q, rotation) + offset_rows)
        .astype(jnp.bfloat16)
        .reshape(rows_q, head_count, 3 * PQ)
    )
    query_sq = jnp.sum(jnp.square(query_pts.astype(jnp.float32)), axis=-1)
    key_sq = jnp.sum(jnp.square(kp_all.astype(jnp.float32)), axis=-1)
    pair_bias = product("hc,qkc->qhk", bias_weight, pair)
    distance = (
        query_sq[:, :, None]
        + jnp.transpose(key_sq)[None, :, :]
        - 2.0 * product("qhe,khe->qhk", query_pts, kp_all)
    )
    logits = LOGIT_SCALE * (
        product("qhc,khc->qhk", query_b, keys_all) / math.sqrt(C)
        + pair_bias
        - 0.5 * point_gain * distance
    )
    attention = jax.nn.softmax(logits, axis=-1)
    attention_b = attention.astype(jnp.bfloat16)
    attended = product("qhk,khc->qhc", attention_b, values_all)
    point_sum = product("qhk,khe->qhe", attention_b, vp_all).reshape(rows_q, head_count, PV, 3)
    pair_out = product("qhk,qkc->qhc", attention_b, pair)
    local_pts = unrotate(point_sum - offset_rows, rotation)
    lengths = jnp.sqrt(1.0 + jnp.sum(jnp.square(local_pts), axis=-1))
    features = jnp.concatenate(
        [attended, local_pts.reshape(rows_q, head_count, 3 * PV), lengths, pair_out], axis=-1
    )
    features = features.astype(jnp.bfloat16).reshape(rows_q, -1)
    output_part = jnp.dot(features, w_out, preferred_element_type=jnp.float32)
    d_features = jnp.dot(d_out, jnp.transpose(w_out), preferred_element_type=jnp.float32).reshape(
        rows_q, head_count, -1
    )
    d_attended = d_features[:, :, :C].astype(jnp.bfloat16)
    d_local = d_features[:, :, C : C + 3 * PV].reshape(rows_q, head_count, PV, 3)
    d_lengths = d_features[:, :, C + 3 * PV : C + 4 * PV]
    d_pair = d_features[:, :, C + 4 * PV :].astype(jnp.bfloat16)
    d_local = d_local + (d_lengths / lengths)[..., None] * local_pts
    d_points = rotate(d_local, rotation).astype(jnp.bfloat16).reshape(rows_q, head_count, 3 * PV)
    d_attention = (
        product("qhc,khc->qhk", d_attended, values_all)
        + product("qhe,khe->qhk", d_points, vp_all)
        + product("qhc,qkc->qhk", d_pair, pair)
    )
    row_total = jnp.sum(attention * d_attention, axis=-1, keepdims=True)
    score_b = (LOGIT_SCALE * attention * (d_attention - row_total)).astype(jnp.bfloat16)
    d_query = product("qhk,khc->qhc", score_b, keys_all) / math.sqrt(C)
    score_rows = jnp.sum(score_b.astype(jnp.float32), axis=-1)[:, :, None]
    d_qpts = point_gain * (
        product("qhk,khe->qhe", score_b, kp_all) - score_rows * query_pts.astype(jnp.float32)
    )
    d_qlocal = (
        unrotate(d_qpts.reshape(rows_q, head_count, PQ, 3), rotation)
        .astype(jnp.bfloat16)
        .reshape(rows_q, -1)
    )
    grad_part = jnp.dot(
        d_query.astype(jnp.bfloat16).reshape(rows_q, -1),
        jnp.transpose(w_query),
        preferred_element_type=jnp.float32,
    )
    grad_part = grad_part + jnp.dot(
        d_qlocal, jnp.transpose(w_query_points), preferred_element_type=jnp.float32
    )
    query_side = jnp.concatenate(
        [
            query_b.reshape(rows_q, -1),
            query_pts.reshape(rows_q, -1),
            d_attended.reshape(rows_q, -1),
            d_points.reshape(rows_q, -1),
        ],
        axis=1,
    )
    return (output_part, grad_part, query_side, attention_b, score_b)


def key_terms(attention_b, score_b, query_side, key_points, point_gain, head_count):
    count_q = query_side.shape[0]
    count_k = key_points.shape[0]
    side_parts = split_columns(
        query_side, [head_count * C, head_count * 3 * PQ, head_count * C, head_count * 3 * PV], 1
    )
    query_b = side_parts[0].reshape(count_q, head_count, C)
    query_pts = side_parts[1].reshape(count_q, head_count, 3 * PQ)
    grad_att = side_parts[2].reshape(count_q, head_count, C)
    grad_pts = side_parts[3].reshape(count_q, head_count, 3 * PV)
    d_key = product("qhk,qhc->khc", score_b, query_b) / math.sqrt(C)
    score_sum = jnp.sum(score_b.astype(jnp.float32), axis=0)
    d_kpts = point_gain * (
        product("qhk,qhe->khe", score_b, query_pts)
        - jnp.transpose(score_sum)[:, :, None] * key_points.astype(jnp.float32)
    )
    d_value = product("qhk,qhc->khc", attention_b, grad_att)
    d_vpts = product("qhk,qhe->khe", attention_b, grad_pts)
    return jnp.concatenate(
        [
            d_key.reshape(count_k, -1),
            d_value.reshape(count_k, -1),
            d_kpts.reshape(count_k, -1),
            d_vpts.reshape(count_k, -1),
        ],
        axis=1,
    )


def key_finish(key_rows, key_frames, w_key, w_value, w_key_points, w_value_points, head_count):
    rows_k = key_rows.shape[0]
    rotation, offset = frame_parts(key_frames)
    pieces = split_columns(
        key_rows, [head_count * C, head_count * C, head_count * 3 * PQ, head_count * 3 * PV], 1
    )
    kp_local = (
        unrotate(pieces[2].reshape(rows_k, head_count, PQ, 3), rotation)
        .astype(jnp.bfloat16)
        .reshape(rows_k, -1)
    )
    vp_local = (
        unrotate(pieces[3].reshape(rows_k, head_count, PV, 3), rotation)
        .astype(jnp.bfloat16)
        .reshape(rows_k, -1)
    )
    result = jnp.dot(
        pieces[0].astype(jnp.bfloat16), jnp.transpose(w_key), preferred_element_type=jnp.float32
    )
    result = result + jnp.dot(
        pieces[1].astype(jnp.bfloat16), jnp.transpose(w_value), preferred_element_type=jnp.float32
    )
    result = result + jnp.dot(
        kp_local, jnp.transpose(w_key_points), preferred_element_type=jnp.float32
    )
    return result + jnp.dot(
        vp_local, jnp.transpose(w_value_points), preferred_element_type=jnp.float32
    )


def shards(
    query_single,
    key_single,
    pair,
    query_frames,
    key_frames,
    w_query,
    w_key,
    w_value,
    w_query_points,
    w_key_points,
    w_value_points,
    head_weight,
    bias_weight,
    w_out,
    d_out,
):
    head_count = head_weight.shape[0]
    keys_b, values_b, key_pts, value_pts = key_side(
        key_single, key_frames, w_key, w_value, w_key_points, w_value_points, head_count
    )
    packed = jnp.concatenate([keys_b, values_b, key_pts, value_pts], axis=1)
    gathered = lax.all_gather(packed, "row", axis=0, tiled=True)
    total_keys = gathered.shape[0]
    pieces = split_columns(
        gathered, [head_count * C, head_count * C, head_count * 3 * PQ, head_count * 3 * PV], 1
    )
    keys_all = pieces[0].reshape(total_keys, head_count, C)
    values_all = pieces[1].reshape(total_keys, head_count, C)
    kp_all = pieces[2].reshape(total_keys, head_count, 3 * PQ)
    vp_all = pieces[3].reshape(total_keys, head_count, 3 * PV)
    output_part, grad_part, query_side, attention_b, score_b = query_pass(
        query_single,
        pair,
        query_frames,
        w_query,
        w_query_points,
        head_weight,
        bias_weight,
        w_out,
        d_out,
        keys_all,
        values_all,
        kp_all,
        vp_all,
    )
    output = lax.psum(output_part, "head").astype(jnp.bfloat16)
    point_gain = (jax.nn.softplus(head_weight) * point_scale(PQ))[None, :, None]
    key_rows = lax.psum_scatter(
        key_terms(attention_b, score_b, query_side, kp_all, point_gain, head_count),
        "row",
        scatter_dimension=0,
        tiled=True,
    )
    grad_keys_part = key_finish(
        key_rows, key_frames, w_key, w_value, w_key_points, w_value_points, head_count
    )
    grad_query, grad_keys = lax.psum((grad_part, grad_keys_part), "head")
    return (output, grad_query, grad_keys)


def solution(mesh):
    return jax.shard_map(
        shards,
        mesh=mesh,
        in_specs=(
            P("row", None),
            P("row", None),
            P("row", None, None),
            P(None, "row"),
            P(None, "row"),
            P(None, "head"),
            P(None, "head"),
            P(None, "head"),
            P(None, "head"),
            P(None, "head"),
            P(None, "head"),
            P("head"),
            P("head", None),
            P("head", None),
            P("row", None),
        ),
        out_specs=(P("row", None), P("row", None), P("row", None)),
        check_vma=False,
    )
```

profile of v0, /device:TPU:1, one launch (start us, length us, event | category | flops | bytes accessed | tf_op | source)
XLA Modules:
  0.0 965.9 jit_solution(1172671194856523547)
XLA Ops:
  14.7 7.5 fusion.10
  29.6 110.6 %all-gather.2.cloned.1.call-done = bf16[8192,204]{1,0:T(8,128)(2,1)} async-done(((bf16[64,204]{1,0:T(8,128)(2,1)}), bf16[8192,204]{1,0:T(8,128)(2,1)}) %all-gather.2.cloned.1.call-update) | async-done | bytes 3342352 | tf_op jit(solution)/shard_map/all_gather | solution.py:248
  140.2 4.2 slice.71
  144.4 2.8 copy.75
  149.7 3.5 slice.72
  153.2 3.8 copy.130
  157.0 4.9 fusion.59
  161.9 2.6 copy.129
  165.9 1.8 fusion.61
  170.1 1.6 fusion.60
  172.4 1.4 convolution_convert_fusion.5
  177.9 2.6 copy.128
  180.6 1.6 fusion.67
  186.4 1.5 fusion.9
  187.9 2.6 reshape.355
  193.1 3.1 pad_maximum_fusion
  196.2 8.7 copy.126
  205.2 1.5 fusion.32
  207.3 1.5 fusion.28
  220.2 606.2 %reduce-scatter.4.cloned.1.call-done = f32[64,204]{1,0:T(8,128)} async-done(((f32[8192,204]{1,0:T(8,128)}), f32[64,204]{1,0:T(8,128)}) %reduce-scatter.4.cloned.1.call-update) | async-done | bytes 52240
  829.6 7.4 convolution_convert_fusion.1
  838.4 102.3 %all-reduce = (bf16[1,384]{1,0:T(2,128)(2,1)}, f32[1,384]{1,0:T(1,128)}) all-reduce(f32[1,384]{1,0:T(1,128)S(1)} %fusion.66, f32[1,384]{1,0:T(1,128)S(1)} %add.118), channel_id=1, replica_groups=mesh['row'=128,'head'=2] {'head'}, use_global_device_ids=true, to_apply=%region_5.6 | all-reduce | flops 768 | bytes 5376 | tf_op jit(solution)/shard_map/psum | solution.py:272
  940.8 17.1 %all-reduce.3.cloned.1.call-done = f32[64,384]{1,0:T(8,128)} async-done(((f32[64,384]{1,0:T(8,128)}), f32[64,384]{1,0:T(8,128)}) %all-reduce.3.cloned.1.call-update) | async-done | bytes 98320 | tf_op jit(solution)/shard_map/psum | solution.py:283
  957.9 1.5 copy.155
  (173 shorter events, 49.1 us)
Async XLA Ops:
  7.2 158.8 %copy-start = (bf16[1,8192,128]{2,1,0:T(8,128)(2,1)S(1)}, bf16[1,8192,128]{2,1,0:T(8,128)(2,1)}, u32[]{:S(2)}) copy-start(bf16[1,8192,128]{2,1,0:T(8,128)(2,1)} %param.17) | copy-start | bytes 6291460
  7.2 133.0 %all-gather.2.cloned.1.call-start = ((), (), s32[]{:S(2)}) async-start(), calls=%async_computation.1 | async-start | bytes 4227072 | tf_op jit(solution)/shard_map/all_gather | solution.py:248
  12.9 10.5 %copy-start.14 = (bf16[384,48]{0,1:T(8,128)(2,1)S(1)}, bf16[384,48]{0,1:T(8,128)(2,1)}, u32[]{:S(2)}) copy-start(bf16[384,48]{0,1:T(8,128)(2,1)} %param.20) | copy-start | bytes 110596
  12.9 10.5 %copy-start.28 = (bf16[1,384]{1,0:T(2,128)(2,1)S(1)}, bf16[1,384]{1,0:T(2,128)(2,1)}, u32[]{:S(2)}) copy-start(bf16[1,384]{1,0:T(2,128)(2,1)} %param.15) | copy-start | bytes 2308
  12.9 10.8 %copy-start.3 = (bf16[528,384]{1,0:T(8,128)(2,1)S(1)}, bf16[528,384]{1,0:T(8,128)(2,1)}, u32[]{:S(2)}) copy-start(bf16[528,384]{1,0:T(8,128)(2,1)} %param.28) | copy-start | bytes 1216516
  12.9 10.8 %copy-start.26 = (bf16[1,384]{1,0:T(2,128)(2,1)S(1)}, bf16[1,384]{1,0:T(2,128)(2,1)}, u32[]{:S(2)}) copy-start(bf16[1,384]{1,0:T(2,128)(2,1)} %param.29) | copy-start | bytes 2308
  13.1 10.9 %copy-start.29 = (f32[12,1]{0,1:T(1,128)S(1)}, f32[12,1]{0,1:T(1,128)}, u32[]{:S(2)}) copy-start(f32[12,1]{0,1:T(1,128)} %param.18) | copy-start | bytes 148
  13.1 11.0 %copy-start.10 = (bf16[384,36]{0,1:T(8,128)(2,1)S(1)}, bf16[384,36]{0,1:T(8,128)(2,1)}, u32[]{:S(2)}) copy-start(bf16[384,36]{0,1:T(8,128)(2,1)} %param.23) | copy-start | bytes 82948
  13.2 15.3 %copy-start.30 = (f32[3]{0:T(128)S(1)}, f32[3]{0:T(128)}, u32[]{:S(2)}) copy-start(f32[3]{0:T(128)} %param.26) | copy-start | bytes 40
  23.2 803.3 %reduce-scatter.4.cloned.1.call-start = ((), (), s32[]{:S(2)}) async-start(), calls=%async_computation.3 | async-start | bytes 8454144
  24.0 120.5 %copy-start.19 = (bf16[1,3,176]{2,1,0:T(4,128)(2,1)}, bf16[1,3,176]{2,1,0:T(4,128)(2,1)S(1)}, u32[]{:S(2)}) copy-start(bf16[1,3,176]{2,1,0:T(4,128)(2,1)S(1)} %copy.152) | copy-start | bytes 3172
  24.0 120.4 %copy-start.15 = (f32[1,3,176]{2,1,0:T(4,128)}, f32[1,3,176]{2,1,0:T(4,128)S(1)}, u32[]{:S(2)}) copy-start(f32[1,3,176]{2,1,0:T(4,128)S(1)} %copy.105) | copy-start | bytes 6340
  24.1 2.3 copy-start.21
  25.1 119.3 %copy-start.16 = (bf16[3,12]{1,0:T(4,128)(2,1)}, bf16[3,12]{1,0:T(4,128)(2,1)S(1)}, u32[]{:S(2)}) copy-start(bf16[3,12]{1,0:T(4,128)(2,1)S(1)} %reshape.340) | copy-start | bytes 220
  161.9 4.0 copy-start.27
  165.9 2.9 copy-start.2
  167.7 1.7 copy-start.25
  180.6 4.2 copy-start.20
  205.0 752.9 %all-reduce.3.cloned.1.call-start = ((), (), s32[]{:S(2)}) async-start(), calls=%async_computation.2 | async-start | bytes 196608 | tf_op jit(solution)/shard_map/psum | solution.py:283
  213.8 613.7 %copy-start.8 = (bf16[384,48]{0,1:T(8,128)(2,1)S(1)}, bf16[384,48]{0,1:T(8,128)(2,1)}, u32[]{:S(2)}) copy-start(bf16[384,48]{0,1:T(8,128)(2,1)} %param.21) | copy-start | bytes 110596
  213.8 613.9 %copy-start.9 = (bf16[384,48]{0,1:T(8,128)(2,1)S(1)}, bf16[384,48]{0,1:T(8,128)(2,1)}, u32[]{:S(2)}) copy-start(bf16[384,48]{0,1:T(8,128)(2,1)} %param.22) | copy-start | bytes 110596
  827.5 9.7 %copy-start.12 = (bf16[384,36]{0,1:T(8,128)(2,1)S(1)}, bf16[384,36]{0,1:T(8,128)(2,1)}, u32[]{:S(2)}) copy-start(bf16[384,36]{0,1:T(8,128)(2,1)} %param.24) | copy-start | bytes 82948
  827.9 9.5 copy-start.7
  828.1 10.2 %copy-start.11 = (bf16[384,36]{0,1:T(8,128)(2,1)S(1)}, bf16[384,36]{0,1:T(8,128)(2,1)}, u32[]{:S(2)}) copy-start(bf16[384,36]{0,1:T(8,128)(2,1)} %param.23) | copy-start | bytes 82948
  (10 other events, 10.8 us)
Sparse Core Ops, SparseCore 0:
  23.3 116.8 all-gather.1
  205.1 621.3 reduce-scatter.3
  838.4 119.4 all-reduce.2
where the time goes:
time: 968 us; the launch traced here: 966 us
  waiting for transfers between devices  734 us (76%)
  blocking collectives  102 us (11%)
  local copies, waits for them, and re-layouts  58.4 us (6%)
  matrix products  40.5 us (4%)
  other arithmetic  15.8 us (2%)
  between operations  14.4 us (1%)
    unnamed x4, waiting for transfers between devices  606 us
    all_gather x1, waiting for transfers between devices, shards(): gathered = lax.all_gather(packed, 'row', axis=0, tiled=True)  111 us
    psum x1, blocking collectives, shards(): output = lax.psum(output_part, 'head').astype(jnp.bfloat16)  102 us
    unnamed x68, local copies, waits for them, and re-layouts  22.5 us
  transfers between devices with their start and end apart: 3, of which 3 were waited for; matrix products, arithmetic and copies ran while one was open for 2% of the time, Pallas kernels for 0%

commit v1 on v0

--- a/solution.py
+++ b/solution.py
@@ -271,11 +271,16 @@
     )
     output = lax.psum(output_part, "head").astype(jnp.bfloat16)
     point_gain = (jax.nn.softplus(head_weight) * point_scale(PQ))[None, :, None]
-    key_rows = lax.psum_scatter(
-        key_terms(attention_b, score_b, query_side, kp_all, point_gain, head_count),
-        "row",
-        scatter_dimension=0,
-        tiled=True,
+    scores = jnp.concatenate([attention_b, score_b], axis=1)
+    rows_n = lax.axis_size("row")
+    local_k = key_single.shape[0]
+    scores = scores.reshape(2 * head_count, rows_n, local_k)
+    scores = lax.all_to_all(scores, "row", split_axis=1, concat_axis=1, tiled=True)
+    scores = jnp.transpose(scores, (1, 0, 2))
+    side_all = lax.all_gather(query_side, "row", axis=0, tiled=True)
+    key_rows = key_terms(
+        scores[:, :head_count], scores[:, head_count:], side_all,
+        key_pts.reshape(local_k, head_count, 3 * PQ), point_gain, head_count,
     )
     grad_keys_part = key_finish(
         key_rows, key_frames, w_key, w_value, w_key_points, w_value_points, head_count

time: 968 us -> 623 us (0.64)
  waiting for transfers between devices: 734 us -> 135 us
  blocking collectives: 102 us -> 369 us
  other arithmetic: 15.8 us -> 5.89 us
    unnamed x4 -> x2, waiting for transfers between devices: 606 us -> 0.03 us
    all_gather x0 -> x1, blocking collectives: none -> 304 us  [shards(): side_all = lax.all_gather(query_side, 'row', axis=0, tiled=True)]
    psum x1, blocking collectives: 102 us -> 65.1 us  [shards(): output = lax.psum(output_part, 'head').astype(jnp.bfloat16)]
    unnamed x68, local copies, waits for them, and re-layouts: 22.5 us -> 11.9 us
where the time goes in v1:
time: 623 us; the launch traced here: 622 us
  blocking collectives  369 us (59%)
  waiting for transfers between devices  135 us (22%)
  local copies, waits for them, and re-layouts  50.5 us (8%)
  matrix products  40.5 us (7%)
  between operations  14.7 us (2%)
  starting transfers between devices  6.41 us (1%)
    all_gather x1, blocking collectives, shards(): side_all = lax.all_gather(query_side, 'row', axis=0, tiled=True)  304 us
    all_gather x1, waiting for transfers between devices, shards(): gathered = lax.all_gather(packed, 'row', axis=0, tiled=True)  108 us
    psum x1, blocking collectives, shards(): output = lax.psum(output_part, 'head').astype(jnp.bfloat16)  65.1 us
    slice x7, local copies, waits for them, and re-layouts, split_columns(): lax.slice_in_dim(packed, cursor, cursor + extent, axis=axis_index)  19 us
    psum x1, waiting for transfers between devices, shards(): grad_query, grad_keys = lax.psum((grad_part, grad_keys_part), 'head')  18.1 us
    dot_general x15, matrix products, product(): return jnp.einsum(form, former, latter, preferred_element_type=jnp.float32)  13.8 us
  transfers between devices with their start and end apart: 3, of which 3 were waited for; matrix products, arithmetic and copies ran while one was open for 2% of the time, Pallas kernels for 0%

profile of v1, /device:TPU:1, one launch (start us, length us, event | category | flops | bytes accessed | tf_op | source)
XLA Modules:
  0.0 621.8 jit_solution(9938110551300458424)
XLA Ops:
  10.2 7.5 %fusion.65 = f32[64,3,4,3]{2,3,1,0:T(4,128)S(1)} fusion(f32[64,3,4,3]{3,2,1,0:T(4,128)S(1)} %copy.139, f32[3,3,64,1]{0,1,3,2:T(4,128)S(1)} %copy.198), kind=kOutput, calls=%fused_computation.113 | convolution fusion | flops 82944 | bytes 20736 | tf_op jit(solution)/shard_map/xyn,nhpy->nhpx/dot_general | solution.py:30
  31.2 108.1 %all-gather.3.cloned.1.call-done = bf16[8192,204]{1,0:T(8,128)(2,1)} async-done(((bf16[64,204]{1,0:T(8,128)(2,1)}), bf16[8192,204]{1,0:T(8,128)(2,1)}) %all-gather.3.cloned.1.call-update) | async-done | bytes 3342352 | tf_op jit(solution)/shard_map/all_gather | solution.py:248
  139.3 4.2 slice.77
  143.5 2.9 copy.151
  149.0 4.9 fusion.59
  153.8 2.7 copy.211
  157.9 1.7 fusion.63
  160.6 3.6 slice.78
  164.2 3.8 copy.212
  167.9 1.7 fusion.29
  171.0 1.6 fusion.61
  173.4 1.4 convolution_convert_fusion.6
  179.6 304.1 %all-gather = bf16[128,1,204]{2,1,0:T(2,128)(2,1)} all-gather(bf16[1,1,204]{2,1,0:T(2,128)(2,1)S(1)} %maximum_bitcast_fusion), channel_id=1, replica_groups=mesh['row'=128,'head'=2] {'row'}, dimensions={0}, use_global_device_ids=true | all-gather | bytes 52632 | tf_op jit(solution)/shard_map/all_gather | solution.py:280
  483.6 1.6 copy.163
  487.9 2.2 fusion.70
  490.1 2.6 copy.210
  492.8 1.4 fusion.50
  494.2 1.8 fusion.20
  500.3 6.1 all-to-all-start
  509.0 8.4 %all-to-all-done = bf16[128,2,192]{2,1,0:T(2,128)(2,1)S(1)} async-done(((bf16[128,2,192]{2,1,0:T(2,128)(2,1)}), bf16[128,2,192]{2,1,0:T(2,128)(2,1)S(1)}, u32[]{:S(2)}, u32[]{:S(2)}) %all-to-all-start) | async-done | bytes 98336 | tf_op jit(solution)/shard_map/all_to_all | solution.py:278
  520.6 7.4 %convolution_convert_fusion.1 = bf16[64,3,4,3]{2,3,1,0:T(4,128)(2,1)S(1)} fusion(f32[64,3,4,3]{3,2,1,0:T(4,128)S(1)} %copy.169, f32[3,3,64,1]{0,1,3,2:T(4,128)S(1)} %copy.198), kind=kOutput, calls=%fused_computation.12 | convolution fusion | flops 85248 | bytes 16128 | tf_op jit(solution)/shard_map/xyn,nhpx->nhpy/dot_general | solution.py:34
  530.2 65.1 %all-reduce = (bf16[1,384]{1,0:T(2,128)(2,1)}, f32[1,384]{1,0:T(1,128)}) all-reduce(f32[1,384]{1,0:T(1,128)S(1)} %fusion.69, f32[1,384]{1,0:T(1,128)S(1)} %add.116), channel_id=1, replica_groups=mesh['row'=128,'head'=2] {'head'}, use_global_device_ids=true, to_apply=%region_5.6 | all-reduce | flops 768 | bytes 5376 | tf_op jit(solution)/shard_map/psum | solution.py:272
  595.2 18.1 %all-reduce.3.cloned.1.call-done = f32[64,384]{1,0:T(8,128)} async-done(((f32[64,384]{1,0:T(8,128)}), f32[64,384]{1,0:T(8,128)}) %all-reduce.3.cloned.1.call-update) | async-done | bytes 98320 | tf_op jit(solution)/shard_map/psum | solution.py:288
  613.4 1.5 copy.242
  (177 shorter events, 42.6 us)
Async XLA Ops:
  7.2 150.7 %copy-start = (bf16[1,8192,128]{2,1,0:T(8,128)(2,1)S(1)}, bf16[1,8192,128]{2,1,0:T(8,128)(2,1)}, u32[]{:S(2)}) copy-start(bf16[1,8192,128]{2,1,0:T(8,128)(2,1)} %param.17) | copy-start | bytes 6291460
  7.2 10.8 %copy-start.4 = (bf16[64,384]{1,0:T(8,128)(2,1)S(1)}, bf16[64,384]{1,0:T(8,128)(2,1)}, u32[]{:S(2)}) copy-start(bf16[64,384]{1,0:T(8,128)(2,1)} %param.16) | copy-start | bytes 147460
  7.2 10.8 %copy-start.6 = (bf16[384,72]{0,1:T(8,128)(2,1)S(1)}, bf16[384,72]{0,1:T(8,128)(2,1)}, u32[]{:S(2)}) copy-start(bf16[384,72]{0,1:T(8,128)(2,1)} %param.25) | copy-start | bytes 165892
  7.2 132.1 %all-gather.3.cloned.1.call-start = ((), (), s32[]{:S(2)}) async-start(), calls=%async_computation.1 | async-start | bytes 4227072 | tf_op jit(solution)/shard_map/all_gather | solution.py:248
  8.8 13.5 %copy-start.3 = (bf16[528,384]{1,0:T(8,128)(2,1)S(1)}, bf16[528,384]{1,0:T(8,128)(2,1)}, u32[]{:S(2)}) copy-start(bf16[528,384]{1,0:T(8,128)(2,1)} %param.28) | copy-start | bytes 1216516
  8.8 13.5 %copy-start.25 = (bf16[1,384]{1,0:T(2,128)(2,1)S(1)}, bf16[1,384]{1,0:T(2,128)(2,1)}, u32[]{:S(2)}) copy-start(bf16[1,384]{1,0:T(2,128)(2,1)} %param.29) | copy-start | bytes 2308
  9.9 12.7 %copy-start.29 = (f32[12,1]{0,1:T(1,128)S(1)}, f32[12,1]{0,1:T(1,128)}, u32[]{:S(2)}) copy-start(f32[12,1]{0,1:T(1,128)} %param.18) | copy-start | bytes 148
  10.1 13.4 %copy-start.28 = (bf16[1,384]{1,0:T(2,128)(2,1)S(1)}, bf16[1,384]{1,0:T(2,128)(2,1)}, u32[]{:S(2)}) copy-start(bf16[1,384]{1,0:T(2,128)(2,1)} %param.15) | copy-start | bytes 2308
  10.1 20.5 %copy-start.30 = (f32[3]{0:T(128)S(1)}, f32[3]{0:T(128)}, u32[]{:S(2)}) copy-start(f32[3]{0:T(128)} %param.26) | copy-start | bytes 40
  22.5 121.0 %copy-start.16 = (f32[1,3,176]{2,1,0:T(4,128)}, f32[1,3,176]{2,1,0:T(4,128)S(1)}, u32[]{:S(2)}) copy-start(f32[1,3,176]{2,1,0:T(4,128)S(1)} %copy.189) | copy-start | bytes 6340
  22.6 121.0 %copy-start.18 = (bf16[1,3,176]{2,1,0:T(4,128)(2,1)}, bf16[1,3,176]{2,1,0:T(4,128)(2,1)S(1)}, u32[]{:S(2)}) copy-start(bf16[1,3,176]{2,1,0:T(4,128)(2,1)S(1)} %copy.237) | copy-start | bytes 3172
  27.2 116.3 %copy-start.24 = (bf16[48]{0:T(256)(128)(2,1)}, bf16[48]{0:T(256)(128)(2,1)S(1)}, u32[]{:S(2)}) copy-start(bf16[48]{0:T(256)(128)(2,1)S(1)} %fusion.18) | copy-start | bytes 292
  498.6 8.3 %copy-start.15 = (f32[3,3]{1,0:T(4,128)S(1)}, f32[3,3]{1,0:T(4,128)}, u32[]{:S(2)}) copy-start(f32[3,3]{1,0:T(4,128)} %reshape.334) | copy-start | bytes 112
  498.6 8.9 %copy-start.14 = (bf16[384,48]{0,1:T(8,128)(2,1)S(1)}, bf16[384,48]{0,1:T(8,128)(2,1)}, u32[]{:S(2)}) copy-start(bf16[384,48]{0,1:T(8,128)(2,1)} %param.20) | copy-start | bytes 110596
  498.6 9.0 %copy-start.17 = (bf16[3,8,3]{1,2,0:T(4,128)(2,1)S(1)}, bf16[3,8,3]{1,2,0:T(4,128)(2,1)}, u32[]{:S(2)}) copy-start(bf16[3,8,3]{1,2,0:T(4,128)(2,1)} %get-tuple-element.15) | copy-start | bytes 436
  499.2 20.9 %copy-start.12 = (f32[64,3,4,3]{0,1,3,2:T(4,128)S(1)}, f32[64,3,4,3]{0,1,3,2:T(4,128)}, u32[]{:S(2)}) copy-start(f32[64,3,4,3]{0,1,3,2:T(4,128)} %copy.166) | copy-start | bytes 27652
  499.2 20.9 %copy-start.22 = (f32[3]{0:T(128)S(1)}, f32[3]{0:T(128)}, u32[]{:S(2)}) copy-start(f32[3]{0:T(128)} %get-tuple-element.5) | copy-start | bytes 40
  500.3 17.1 %all-to-all-start = ((bf16[128,2,192]{2,1,0:T(2,128)(2,1)}), bf16[128,2,192]{2,1,0:T(2,128)(2,1)S(1)}, u32[]{:S(2)}, u32[]{:S(2)}) async-start(bf16[128,2,192]{2,1,0:T(2,128)(2,1)} %reshape.419), calls=%async_computation | async-start | bytes 262144 | tf_op jit(solution)/shard_map/all_to_all | solution.py:278
  506.4 107.0 %all-reduce.3.cloned.1.call-start = ((), (), s32[]{:S(2)}) async-start(), calls=%async_computation.2 | async-start | bytes 196608 | tf_op jit(solution)/shard_map/psum | solution.py:288
  508.2 20.3 %copy-start.8 = (bf16[384,48]{0,1:T(8,128)(2,1)S(1)}, bf16[384,48]{0,1:T(8,128)(2,1)}, u32[]{:S(2)}) copy-start(bf16[384,48]{0,1:T(8,128)(2,1)} %param.21) | copy-start | bytes 110596
  509.0 19.7 %copy-start.9 = (bf16[384,48]{0,1:T(8,128)(2,1)S(1)}, bf16[384,48]{0,1:T(8,128)(2,1)}, u32[]{:S(2)}) copy-start(bf16[384,48]{0,1:T(8,128)(2,1)} %param.22) | copy-start | bytes 110596
  517.5 11.4 %copy-start.11 = (bf16[384,36]{0,1:T(8,128)(2,1)S(1)}, bf16[384,36]{0,1:T(8,128)(2,1)}, u32[]{:S(2)}) copy-start(bf16[384,36]{0,1:T(8,128)(2,1)} %param.24) | copy-start | bytes 82948
  517.5 11.6 %copy-start.7 = (bf16[384,72]{0,1:T(8,128)(2,1)S(1)}, bf16[384,72]{0,1:T(8,128)(2,1)}, u32[]{:S(2)}) copy-start(bf16[384,72]{0,1:T(8,128)(2,1)} %param.25) | copy-start | bytes 165892
  518.7 11.3 %copy-start.10 = (bf16[384,36]{0,1:T(8,128)(2,1)S(1)}, bf16[384,36]{0,1:T(8,128)(2,1)}, u32[]{:S(2)}) copy-start(bf16[384,36]{0,1:T(8,128)(2,1)} %param.23) | copy-start | bytes 82948
  (10 other events, 59.1 us)
Sparse Core Ops, SparseCore 0:
  22.4 116.8 all-gather.2
  530.1 83.2 all-reduce.2

commit v2 on v0

v2 whole, which is shorter than its diff:
```python
import functools
import math

import jax
import jax.numpy as jnp
from jax import lax
from jax.experimental import pallas as pl
from jax.experimental.pallas import tpu as pltpu
from jax.sharding import PartitionSpec as P

NY, NZ, NX = 4, 8, 4
ROWS = NY * NZ * NX
LK = 64
K = ROWS * LK
SIZES = (NY, NZ, NX)
LOGIT_SCALE = math.sqrt(1.0 / 3.0)
POINT_SCALE = math.sqrt(2.0 / 36.0)
MESH = pl.DeviceIdType.MESH
BF, F32 = jnp.bfloat16, jnp.float32

STREAMS = (
    (0, 0, 16, (2, 0, 1)),
    (0, 16, 32, (0, 1, 2)),
    (0, 48, 16, (1, 2, 0)),
    (1, 0, 16, (2, 0, 1)),
    (1, 16, 16, (0, 1, 2)),
    (1, 32, 32, (1, 2, 0)),
)
ROUNDS = 8


def nt(a, b):
    return lax.dot_general(a, b, (((1,), (1,)), ((), ())), preferred_element_type=F32)


def nn(a, b):
    return lax.dot_general(a, b, (((1,), (0,)), ((), ())), preferred_element_type=F32)


def tn(a, b, precision=None):
    return lax.dot_general(
        a, b, (((0,), (0,)), ((), ())), preferred_element_type=F32, precision=precision
    )


def iotas(shape):
    return (
        lax.broadcasted_iota(jnp.int32, shape, 0),
        lax.broadcasted_iota(jnp.int32, shape, 1),
    )


def third(value):
    return lax.shift_right_logical(value * 43, 7)


def within(lane, start, count):
    return (lane >= start) & (lane < start + count)


SHIFTS = (0, 1, 2, -1, -2)


def selection():
    j, l = iotas((12, 128))
    x = l - 3 * third(l)
    parts = []
    for d in SHIFTS:
        ok = (x + d >= 0) & (x + d < 3)
        parts.append(ok & (j == 4 * x + d))
    parts.append(j == 9 + x)
    for d in SHIFTS[1:]:
        ok = (x + d >= 0) & (x + d < 3)
        parts.append(ok & (j == 4 * x + 3 * d))
    return jnp.concatenate([jnp.where(p, 1.0, 0.0) for p in parts], axis=1)


def part(pat, i):
    return pat[:, 128 * i : 128 * i + 128]


def shifted(v, d):
    return v if d == 0 else pltpu.roll(v, (-d) % 128, 1)


def rotated(v, pat):
    return sum(part(pat, i) * shifted(v, d) for i, d in enumerate(SHIFTS))


def unrotated(v, pat):
    out = part(pat, 0) * v
    for i, d in enumerate(SHIFTS[1:]):
        out = out + part(pat, 6 + i) * shifted(v, d)
    return out


def softplus(x):
    return jnp.maximum(x, 0.0) + jnp.log1p(jnp.exp(-jnp.abs(x)))


def by_head(index, values):
    return jnp.where(index == 0, values[0], jnp.where(index == 1, values[1], values[2]))


def mask_k(r, l):
    return within(l, 16 * r, 16) & (r < 3), within(l, 48 + 12 * r, 12) & (r < 3)


def mask_v(r, l):
    return (within(l, 16 * r, 16) | within(l, 48 + 24 * r, 24)) & (r < 3)


def kernel(
    qs, ks, pair, qfr, kfr, w_q, w_k, w_v, w_qp, w_kp, w_vp, hw, bw, w_o, d_o,
    o_out, o_gq, o_gk,
    buf_k, buf_v, pair_s, wq_s, wk_s, wv_s, wp_s, lhs_s, pb_s, att_s, da_s, msg, recv, recv_f,
    pat_s, part_s, got_s,
    pair_sem, send_sem, recv_sem, a2a_send, a2a_recv, own_sem, ex_send, ex_recv,
):
    row = lax.axis_index("row")
    core = lax.axis_index("head")
    coords = (row // (NZ * NX), (row // NX) % NZ, row % NX)

    def neighbour(axis, step):
        moved = list(coords)
        moved[axis] = (coords[axis] + step + SIZES[axis]) % SIZES[axis]
        return (moved[0] * NZ + moved[1]) * NX + moved[2]

    barrier = pltpu.get_barrier_semaphore()
    for axis in range(3):
        for step in (1, -1):
            pl.semaphore_signal(
                barrier, inc=1, device_id=(neighbour(axis, step), core), device_id_type=MESH
            )
    pl.semaphore_signal(barrier, inc=1, device_id=(row, 1 - core), device_id_type=MESH)
    pair_copy = pltpu.make_async_copy(pair.at[0], pair_s, pair_sem)
    pair_copy.start()

    wk_s[...] = jnp.zeros_like(wk_s)
    wk_s[:, 0:48] = w_k[...]
    wk_s[:, 48:84] = w_kp[...]
    wv_s[...] = jnp.zeros_like(wv_s)
    wv_s[:, 0:48] = w_v[...]
    wv_s[:, 48:120] = w_vp[...]
    select = selection()
    pat = tn(kfr[...], select, lax.Precision.HIGHEST)
    pat_s[...] = pat
    r64, l64 = iotas((LK, 128))
    feat = nn(ks[...], wk_s[...])
    k_rows = jnp.where(
        l64 < 48, feat, jnp.where(l64 < 84, rotated(feat, pat) + part(pat, 5), 0.0)
    ).astype(BF)
    k_full = k_rows.astype(F32)
    square = k_full * k_full
    for h in range(3):
        total = jnp.sum(
            jnp.where(within(l64, 48 + 12 * h, 12), square, 0.0), axis=1, keepdims=True
        )
        high = total.astype(BF).astype(F32)
        middle = (total - high).astype(BF).astype(F32)
        low = total - high - middle
        at = 84 + 3 * h
        k_full = jnp.where(
            l64 == at, high, jnp.where(l64 == at + 1, middle, jnp.where(l64 == at + 2, low, k_full))
        )
    feat = nn(ks[...], wv_s[...])
    v_rows = jnp.where(
        l64 < 48, feat, jnp.where(l64 < 120, rotated(feat, pat) + part(pat, 5), 0.0)
    ).astype(BF)
    mine = (pl.ds(coords[0], 1), pl.ds(coords[1], 1), pl.ds(coords[2], 1))
    buf_k[mine] = k_full.astype(BF).reshape(1, 1, 1, LK, 128)
    buf_v[mine] = v_rows.reshape(1, 1, 1, LK, 128)

    bufs = (buf_k, buf_v)

    def copies(s, rnd):
        which, first, count, order = STREAMS[s]
        left = rnd
        for phase, axis in enumerate(order):
            rounds = SIZES[axis] // 2
            if left < rounds:
                break
            left -= rounds
        out = []
        for direction, step in enumerate((1, -1)):
            at = [pl.ds(c, 1) for c in coords]
            for done in order[:phase]:
                at[done] = pl.ds(0, SIZES[done])
            at[axis] = pl.ds((coords[axis] - step * left + SIZES[axis]) % SIZES[axis], 1)
            if left == rounds - 1:
                if phase == 0:
                    if direction != s % 2:
                        continue
                else:
                    split = order[0]
                    at[split] = pl.ds(direction * (SIZES[split] // 2), SIZES[split] // 2)
            where = bufs[which].at[at[0], at[1], at[2], pl.ds(first, count)]
            out.append(
                pltpu.make_async_remote_copy(
                    src_ref=where,
                    dst_ref=where,
                    send_sem=send_sem.at[s, rnd, direction],
                    recv_sem=recv_sem.at[s, rnd, direction],
                    device_id=(neighbour(axis, step), core),
                    device_id_type=MESH,
                )
            )
        return out

    pl.semaphore_wait(barrier, 7)

    def start_round(s, rnd):
        for copy in copies(s, rnd):
            copy.start()

    def end_round(s, rnd):
        for copy in copies(s, rnd):
            copy.wait_recv()

    for s in range(6):
        start_round(s, 0)

    wq_s[...] = jnp.zeros_like(wq_s)
    wq_s[:, 0:48] = w_q[...]
    wq_s[:, 48:84] = w_qp[...]
    pat_q = tn(qfr[...], select, lax.Precision.HIGHEST)
    _, l1 = iotas((1, 128))
    x1 = l1 - 3 * third(l1)
    feat = nn(qs[...], wq_s[...])
    q_row = jnp.where(
        l1 < 48, feat, jnp.where(l1 < 84, rotated(feat, pat_q) + part(pat_q, 5), 0.0)
    )
    q_row = q_row.astype(BF).astype(F32)
    r8, l8 = iotas((8, 128))
    raw = [hw[0], hw[1], hw[2]]
    gain = (softplus(by_head(r8, raw)) * POINT_SCALE)[:, 0:1]
    keys8, points8 = mask_k(r8, l8)
    values8 = mask_v(r8, l8)
    q8 = jnp.broadcast_to(q_row, (8, 128))
    q_square = jnp.sum(jnp.where(points8, q8 * q8, 0.0), axis=1, keepdims=True)
    lhs_q = jnp.concatenate(
        [
            jnp.where(keys8, q8, 0.0),
            jnp.where(points8, q8, jnp.where(within(l8, 84 + 3 * r8, 3) & (r8 < 3), -0.5, 0.0)),
        ],
        axis=0,
    ).astype(BF)

    i256, _ = iotas((256, 1))
    i = i256 & 127
    j = i - 48
    head = lax.shift_right_logical(j * 43, 10)
    point = third(j)
    p_head = lax.shift_right_logical(point, 3)
    source = jnp.where(
        i256 < 128,
        jnp.where(i < 48, 176 * lax.shift_right_logical(i, 4) + (i & 15), 152 * head + 16 + j),
        176 * p_head + 40 + (point & 7),
    )
    valid = (i < 120) & ((i256 < 128) | (i >= 48))
    source = jnp.where(valid, source, -1)
    _, lane_o = iotas((256, 528))
    pick = jnp.where(lane_o == source, 1.0, 0.0).astype(BF)
    wp_s[...] = nn(pick, w_o[...]).astype(BF)
    d_feat = nt(d_o[...], wp_s[...])
    lhs_s[...] = jnp.zeros_like(lhs_s)
    lhs_s[0:3, :] = bw[...].astype(F32)
    for h in range(3):
        lhs_s[8 + h : 9 + h, :] = nt(d_o[...], w_o[176 * h + 48 : 176 * h + 176, :])
    lhs_p = lhs_s[...].astype(BF)
    pair_copy.wait()

    def pair_step(g, _):
        at = pl.multiple_of(g * 1024, 1024)
        pb_s[:, pl.ds(at, 1024)] = nt(lhs_p, pair_s[pl.ds(at, 1024), :])
        return 0

    for rnd in range(1, ROUNDS + 1):
        lax.fori_loop(rnd - 1, rnd, pair_step, 0)
        for s in range(6):
            end_round(s, rnd - 1)
            if rnd < ROUNDS:
                start_round(s, rnd)

    def chunk(ref, g):
        return ref[pl.ds(g // 2, 1), pl.ds((g % 2) * 4, 4)].reshape(1024, 128)

    def logit_step(g, top):
        at = pl.multiple_of(g * 1024, 1024)
        both = nt(lhs_q, chunk(buf_k, g))
        logits = LOGIT_SCALE * (
            both[0:8] * 0.25
            + pb_s[0:8, pl.ds(at, 1024)]
            + gain * (both[8:16] - 0.5 * q_square)
        )
        att_s[:, pl.ds(at, 1024)] = logits
        return jnp.maximum(top, jnp.max(logits, axis=1, keepdims=True))

    top = lax.fori_loop(0, 8, logit_step, jnp.full((8, 1), -3.0e38, F32))

    def exp_step(g, total):
        at = pl.multiple_of(g * 1024, 1024)
        e = jnp.exp(att_s[:, pl.ds(at, 1024)] - top)
        att_s[:, pl.ds(at, 1024)] = e
        return total + jnp.sum(e, axis=1, keepdims=True)

    total = lax.fori_loop(0, 8, exp_step, jnp.zeros((8, 1), F32))

    def attend_step(g, carry):
        acc_v, acc_p = carry
        at = pl.multiple_of(g * 1024, 1024)
        a = att_s[:, pl.ds(at, 1024)] / total
        att_s[:, pl.ds(at, 1024)] = a
        a = a.astype(BF)
        return (
            acc_v + nn(a, chunk(buf_v, g)),
            acc_p + nn(a, pair_s[pl.ds(at, 1024), :]),
        )

    zero8 = jnp.zeros((8, 128), F32)
    acc_v, acc_p = lax.fori_loop(0, 8, attend_step, (zero8, zero8))
    row_v = jnp.sum(jnp.where(values8, acc_v, 0.0), axis=0, keepdims=True)
    is_point = within(l1, 48, 72)
    local = jnp.where(is_point, unrotated(jnp.where(is_point, row_v - part(pat_q, 5), 0.0), pat_q), 0.0)
    squares = local * local
    norm = squares
    for d in SHIFTS[1:]:
        norm = norm + jnp.where((x1 + d >= 0) & (x1 + d < 3), shifted(squares, d), 0.0)
    lengths = jnp.sqrt(1.0 + norm)
    f_v = jnp.where(l1 < 48, row_v, local).astype(BF)
    f_len = jnp.where(is_point & (x1 == 0), lengths, 0.0).astype(BF)
    out_row = nn(f_v, wp_s[0:128, :]) + nn(f_len, wp_s[128:256, :])
    for h in range(3):
        out_row = out_row + nn(
            acc_p[h : h + 1, :].astype(BF), w_o[176 * h + 48 : 176 * h + 176, :]
        )
    part_s[64:65, :] = out_row

    d_local = d_feat[:, 0:128] + d_feat[:, 128:256] / lengths * local
    d_local = jnp.where(is_point, d_local, 0.0)
    side_v = jnp.where(
        l1 < 48, d_feat[:, 0:128], jnp.where(is_point, rotated(d_local, pat_q), 0.0)
    )
    side_v8 = jnp.broadcast_to(side_v, (8, 128))
    lhs_v = jnp.where(values8, side_v8, 0.0).astype(BF)

    def grad_step(g, carry):
        at = pl.multiple_of(g * 1024, 1024)
        d_att = nt(lhs_v, chunk(buf_v, g)) + pb_s[8:16, pl.ds(at, 1024)]
        da_s[:, pl.ds(at, 1024)] = d_att
        return carry + jnp.sum(att_s[:, pl.ds(at, 1024)] * d_att, axis=1, keepdims=True)

    row_total = lax.fori_loop(0, 8, grad_step, jnp.zeros((8, 1), F32))
    side = jnp.where(r8 == 6, q8, jnp.where(r8 == 7, side_v8, 0.0))
    side = jnp.concatenate([side] * 8, axis=1)
    rc, _ = iotas((8, 1024))

    def score_step(g, carry):
        acc, sums = carry
        at = pl.multiple_of(g * 1024, 1024)
        a = att_s[:, pl.ds(at, 1024)]
        score = LOGIT_SCALE * a * (da_s[:, pl.ds(at, 1024)] - row_total)
        out = jnp.where(rc < 3, a, jnp.where(rc < 6, pltpu.roll(score, 3, 0), side))
        msg[:, pl.ds(at, 1024)] = out.astype(BF)
        score = score.astype(BF)
        acc = acc + nn(score, chunk(buf_k, g))
        return acc, sums + jnp.sum(score.astype(F32), axis=1, keepdims=True)

    acc_k, score_rows = lax.fori_loop(0, 8, score_step, (zero8, jnp.zeros((8, 1), F32)))

    def tile(device):
        return msg.at[:, pl.ds(pl.multiple_of((device // 2) * 128, 128), 128)]

    def send_step(i, _):
        target = (row + i) % ROWS
        pltpu.make_async_remote_copy(
            src_ref=tile(target),
            dst_ref=recv.at[row],
            send_sem=a2a_send,
            recv_sem=a2a_recv,
            device_id=(target, core),
            device_id_type=MESH,
        ).start()
        return 0

    own = pltpu.make_async_copy(tile(row), recv.at[row], own_sem)
    own.start()
    lax.fori_loop(1, ROWS, send_step, 0)

    q_terms = jnp.where(keys8, acc_k * 0.25, 0.0) + jnp.where(
        points8, gain * (acc_k - score_rows * q8), 0.0
    )
    d_q = jnp.sum(q_terms, axis=0, keepdims=True)
    d_q = jnp.where(l1 < 48, d_q, jnp.where(l1 < 84, unrotated(d_q, pat_q), 0.0)).astype(BF)
    part_s[72:73, :] = nt(d_q, wq_s[...])

    own.wait()
    everyone = recv.at[pl.ds(0, ROWS - 1)]
    pltpu.make_async_copy(everyone, everyone, a2a_recv).wait()

    def unpack_step(i, _):
        at = pl.multiple_of(i * 64, 64)
        recv_f[pl.ds(at, 64), :] = recv[pl.ds(i * 8, 8)].astype(F32).reshape(64, 128)
        return 0

    lax.fori_loop(0, ROWS // 8, unpack_step, 0)

    def every(i):
        return recv_f[pl.ds(i, ROWS, stride=8), :]

    side_k, side_v = every(6), every(7)
    _, l128 = iotas((ROWS, 128))
    out_k = out_v = sums = jnp.zeros((128, 128), F32)
    for h in range(3):
        keys_h = within(l128, 16 * h, 16)
        points_h = within(l128, 48 + 12 * h, 12)
        vpoints_h = within(l128, 48 + 24 * h, 24)
        att_h, score_h = every(h).astype(BF), every(3 + h).astype(BF)
        out_v = out_v + tn(att_h, jnp.where(keys_h | vpoints_h, side_v, 0.0).astype(BF))
        out_k = out_k + tn(score_h, jnp.where(keys_h | points_h, side_k, 0.0).astype(BF))
        sums = sums + tn(score_h, jnp.where(points_h, 1.0, 0.0).astype(BF))
    odd = row % 2 == 1

    def mine_of(x):
        return jnp.where(odd, x[64:128], x[0:64])

    out_k, out_v, sums = mine_of(out_k), mine_of(out_v), mine_of(sums)
    pat = pat_s[...]
    kf = buf_k[mine].reshape(LK, 128).astype(F32)
    gain_l = softplus(by_head(jnp.where(l1 < 60, 0, jnp.where(l1 < 72, 1, 2)), raw)) * POINT_SCALE
    d_points = jnp.where(within(l64, 48, 36), gain_l * (out_k - sums * kf), 0.0)
    d_k = jnp.where(l64 < 48, out_k * 0.25, jnp.where(l64 < 84, unrotated(d_points, pat), 0.0))
    d_v = jnp.where(l64 < 48, out_v, jnp.where(l64 < 120, unrotated(out_v, pat), 0.0))
    part_s[0:64, :] = nt(d_k.astype(BF), wk_s[...]) + nt(d_v.astype(BF), wv_s[...])

    exchange = pltpu.make_async_remote_copy(
        src_ref=part_s,
        dst_ref=got_s,
        send_sem=ex_send,
        recv_sem=ex_recv,
        device_id=(row, 1 - core),
        device_id_type=MESH,
    )
    exchange.start()
    for s in range(6):
        for rnd in range(ROUNDS):
            for copy in copies(s, rnd):
                copy.wait_send()
    pltpu.make_async_copy(everyone, everyone, a2a_send).wait()
    exchange.wait()
    o_gk[...] = part_s[0:64, :] + got_s[0:64, :]
    o_out[...] = (part_s[64:65, :] + got_s[64:65, :]).astype(BF)
    o_gq[...] = part_s[72:73, :] + got_s[72:73, :]


def shards(
    query_single, key_single, pair, query_frames, key_frames, w_query, w_key, w_value,
    w_query_points, w_key_points, w_value_points, head_weight, bias_weight, w_out, d_out,
):
    vmem = pl.BlockSpec(memory_space=pltpu.VMEM)
    specs = [vmem] * 15
    specs[2] = pl.BlockSpec(memory_space=pl.ANY)
    specs[11] = pl.BlockSpec(memory_space=pltpu.SMEM)
    dma = pltpu.SemaphoreType.DMA
    return pl.pallas_call(
        kernel,
        out_shape=(
            jax.ShapeDtypeStruct((1, 384), BF),
            jax.ShapeDtypeStruct((1, 384), F32),
            jax.ShapeDtypeStruct((LK, 384), F32),
        ),
        in_specs=specs,
        out_specs=(vmem, vmem, vmem),
        scratch_shapes=[
            pltpu.VMEM((NY, NZ, NX, LK, 128), BF),
            pltpu.VMEM((NY, NZ, NX, LK, 128), BF),
            pltpu.VMEM((K, 128), BF),
            pltpu.VMEM((384, 128), BF),
            pltpu.VMEM((384, 128), BF),
            pltpu.VMEM((384, 128), BF),
            pltpu.VMEM((256, 384), BF),
            pltpu.VMEM((16, 128), F32),
            pltpu.VMEM((16, K), F32),
            pltpu.VMEM((8, K), F32),
            pltpu.VMEM((8, K), F32),
            pltpu.VMEM((8, K), BF),
            pltpu.VMEM((ROWS, 8, 128), BF),
            pltpu.VMEM((ROWS * 8, 128), F32),
            pltpu.VMEM((LK, 1280), F32),
            pltpu.VMEM((80, 384), F32),
            pltpu.VMEM((80, 384), F32),
            dma, dma((6, ROUNDS, 2)), dma((6, ROUNDS, 2)), dma, dma, dma, dma, dma,
        ],
        compiler_params=pltpu.CompilerParams(
            collective_id=0, has_side_effects=True, vmem_limit_bytes=48 * 1024 * 1024
        ),
    )(
        query_single, key_single, pair, query_frames, key_frames, w_query, w_key, w_value,
        w_query_points, w_key_points, w_value_points, head_weight, bias_weight, w_out, d_out,
    )


def solution(mesh):
    return jax.shard_map(
        shards,
        mesh=mesh,
        in_specs=(
            P("row", None),
            P("row", None),
            P("row", None, None),
            P(None, "row"),
            P(None, "row"),
            P(None, "head"),
            P(None, "head"),
            P(None, "head"),
            P(None, "head"),
            P(None, "head"),
            P(None, "head"),
            P("head"),
            P("head", None),
            P("head", None),
            P("row", None),
        ),
        out_specs=(P("row", None), P("row", None), P("row", None)),
        check_vma=False,
    )
```

time: 968 us -> 81 us (0.08)
  waiting for transfers between devices: 734 us -> 0 us
  blocking collectives: 102 us -> 0 us
  Pallas kernels: 0 us -> 65 us
  local copies, waits for them, and re-layouts: 58.4 us -> 14.6 us
  matrix products: 40.5 us -> 0 us
  other arithmetic: 15.8 us -> 0 us
  between operations: 14.4 us -> 0.68 us
    unnamed x4 -> x0, waiting for transfers between devices: 606 us -> none
    all_gather x1 -> x0, waiting for transfers between devices: 111 us -> none  [shards(): gathered = lax.all_gather(packed, 'row', axis=0, tiled=True)]
    psum x1 -> x0, blocking collectives: 102 us -> none  [shards(): output = lax.psum(output_part, 'head').astype(jnp.bfloat16)]
    pallas_call x0 -> x1, Pallas kernels: none -> 65 us  [shards(): pl.pallas_call(kernel, out_shape=(jax.ShapeDtypeStruct((1, 384), BF), jax...]
    dot_general x33 -> x0, matrix products: 40.5 us -> none  [the longest x11 12.2 us: product(): return jnp.einsum(form, former, latter, preferred_element_type=jnp.float32)]
    psum x1 -> x0, waiting for transfers between devices: 17.1 us -> none  [shards(): grad_query, grad_keys = lax.psum((grad_part, grad_keys_part), 'head')]
    slice x8 -> x0, local copies, waits for them, and re-layouts: 15.5 us -> none  [the longest x6 15.4 us: split_columns(): lax.slice_in_dim(packed, cursor, cursor + extent, axis=axis_index)]
    unnamed x68 -> x26, local copies, waits for them, and re-layouts: 22.5 us -> 14.6 us
  transfers between devices with their start and end apart: 3 -> 0, of which waited for: 3 -> 0; matrix products, arithmetic and copies ran while one was open for 2% -> 0% of each run, Pallas kernels for 0% -> 0%
where the time goes in v2:
time: 81 us; the launch traced here: 80.3 us
  Pallas kernels  65 us (80%)
  local copies, waits for them, and re-layouts  14.6 us (18%)
    pallas_call x1, Pallas kernels, shards(): pl.pallas_call(kernel, out_shape=(jax.ShapeDtypeStruct((1, 384), BF), jax...  65 us
    unnamed x26, local copies, waits for them, and re-layouts  14.6 us

profile of v2, /device:TPU:1, one launch (start us, length us, event | category | flops | bytes accessed | tf_op | source)
XLA Modules:
  0.0 80.3 jit_solution(9545710904779105319)
XLA Ops:
  0.6 0.7 copy.18.qfr
  1.4 0.9 %copy.19.w_q = bf16[384,48]{1,0:T(8,128)(2,1)S(1)} copy(bf16[384,48]{0,1:T(8,128)(2,1)} %param.20) | data formatting | bytes 73728 | tf_op args[5]
  2.3 0.9 %copy.20.w_k = bf16[384,48]{1,0:T(8,128)(2,1)S(1)} copy(bf16[384,48]{0,1:T(8,128)(2,1)} %param.21) | data formatting | bytes 73728 | tf_op args[6]
  3.2 0.9 %copy.21.w_v = bf16[384,48]{1,0:T(8,128)(2,1)S(1)} copy(bf16[384,48]{0,1:T(8,128)(2,1)} %param.22) | data formatting | bytes 73728 | tf_op args[7]
  4.0 0.9 %copy.22.w_qp = bf16[384,36]{1,0:T(8,128)(2,1)S(1)} copy(bf16[384,36]{0,1:T(8,128)(2,1)} %param.23) | data formatting | bytes 55296 | tf_op args[8]
  4.9 0.9 %copy.23.w_kp = bf16[384,36]{1,0:T(8,128)(2,1)S(1)} copy(bf16[384,36]{0,1:T(8,128)(2,1)} %param.24) | data formatting | bytes 55296 | tf_op args[9]
  5.8 0.9 %copy.24.w_vp = bf16[384,72]{1,0:T(8,128)(2,1)S(1)} copy(bf16[384,72]{0,1:T(8,128)(2,1)} %param.25) | data formatting | bytes 110592 | tf_op args[10]
  6.8 0.0 copy-start
  6.8 1.6 %copy-done = bf16[1,8192,128]{2,1,0:T(8,128)(2,1)S(1)} copy-done((bf16[1,8192,128]{2,1,0:T(8,128)(2,1)S(1)}, bf16[1,8192,128]{2,1,0:T(8,128)(2,1)}, u32[]{:S(2)}) %copy-start) | copy-done | bytes 2097176
  8.4 0.0 copy-start.1
  8.4 1.0 %copy-done.1 = bf16[528,384]{1,0:T(8,128)(2,1)S(1)} copy-done((bf16[528,384]{1,0:T(8,128)(2,1)S(1)}, bf16[528,384]{1,0:T(8,128)(2,1)}, u32[]{:S(2)}) %copy-start.1) | copy-done | bytes 405528
  9.4 0.0 copy-start.2
  9.4 0.8 copy-done.2
  10.2 0.0 copy-start.3
  10.2 0.7 copy-done.3
  10.9 0.0 copy-start.4
  10.9 0.7 copy-done.4
  11.5 0.7 copy-done.5
  12.2 0.7 copy-done.6
  12.9 0.7 copy-done.7
  13.6 65.0 %shard_map.166 = (bf16[1,384]{1,0:T(2,128)(2,1)S(1)}, f32[1,384]{1,0:T(1,128)S(1)}, f32[64,384]{1,0:T(8,128)S(1)}) custom-call(bf16[1,384]{1,0:T(2,128)(2,1)S(1)} %copy-done.4, bf16[64,384]{1,0:T(8,128)(2,1)S(1)} %copy-done.2, bf16[1,8192,128]{2,1,0:T(8,128)(2,1)S(1)} %copy-done, f32[12,1]{1,0:T(8,128)S(1)} %copy.18.qfr, f32[12,64]{1,0:T(8,128)S(1)} %copy-done.3, ...), custom_call_target="tpu_custom_call" | custom-call | tf_op jit(solution)/shard_map/pallas_call | solution.py:465
  78.6 0.6 copy.28
  79.1 0.6 copy.29
  79.7 0.6 copy.30
  (3 shorter events, 0.0 us)
Async XLA Ops:
  6.8 1.6 %copy-start = (bf16[1,8192,128]{2,1,0:T(8,128)(2,1)S(1)}, bf16[1,8192,128]{2,1,0:T(8,128)(2,1)}, u32[]{:S(2)}) copy-start(bf16[1,8192,128]{2,1,0:T(8,128)(2,1)} %pair.1) | copy-start | bytes 6291460
  8.4 1.0 %copy-start.1 = (bf16[528,384]{1,0:T(8,128)(2,1)S(1)}, bf16[528,384]{1,0:T(8,128)(2,1)}, u32[]{:S(2)}) copy-start(bf16[528,384]{1,0:T(8,128)(2,1)} %w_o.1) | copy-start | bytes 1216516
  9.4 0.8 copy-start.2
  10.2 0.7 copy-start.3
  10.9 0.7 copy-start.4
  11.5 0.7 copy-start.5
  12.2 0.7 copy-start.6
  12.9 0.7 copy-start.7

commit v3 on v2

--- a/solution.py
+++ b/solution.py
@@ -111,14 +111,28 @@
 
 
 def kernel(
-    qs, ks, pair, qfr, kfr, w_q, w_k, w_v, w_qp, w_kp, w_vp, hw, bw, w_o, d_o,
+    qs_h, ks_h, pair, qfr_h, kfr_h, w_q_h, w_k_h, w_v_h, w_qp_h, w_kp_h, w_vp_h, hw_h, bw_h,
+    w_o_h, d_o_h,
     o_out, o_gq, o_gk,
+    qs, ks, qfr, kfr, w_q, w_k, w_v, w_qp, w_kp, w_vp, hw, bw, w_o, d_o, in_sem,
     buf_k, buf_v, pair_s, wq_s, wk_s, wv_s, wp_s, lhs_s, pb_s, att_s, da_s, msg, recv, recv_f,
     pat_s, part_s, got_s,
     pair_sem, send_sem, recv_sem, a2a_send, a2a_recv, own_sem, ex_send, ex_recv,
 ):
     row = lax.axis_index("row")
     core = lax.axis_index("head")
+    loads = [
+        pltpu.make_async_copy(src, dst, in_sem.at[n])
+        for n, (src, dst) in enumerate(
+            (
+                (ks_h, ks), (kfr_h, kfr), (w_k_h, w_k), (w_kp_h, w_kp), (w_v_h, w_v), (w_vp_h, w_vp),
+                (qs_h, qs), (qfr_h, qfr), (w_q_h, w_q), (w_qp_h, w_qp), (hw_h, hw), (bw_h, bw),
+                (w_o_h, w_o), (d_o_h, d_o),
+            )
+        )
+    ]
+    for load in loads:
+        load.start()
     coords = (row // (NZ * NX), (row // NX) % NZ, row % NX)
 
     def neighbour(axis, step):
@@ -136,17 +150,19 @@
     pair_copy = pltpu.make_async_copy(pair.at[0], pair_s, pair_sem)
     pair_copy.start()
 
+    select = selection()
+    for load in loads[:6]:
+        load.wait()
     wk_s[...] = jnp.zeros_like(wk_s)
-    wk_s[:, 0:48] = w_k[...]
-    wk_s[:, 48:84] = w_kp[...]
+    wk_s[0:48, :] = w_k[...]
+    wk_s[48:84, :] = w_kp[...]
     wv_s[...] = jnp.zeros_like(wv_s)
-    wv_s[:, 0:48] = w_v[...]
-    wv_s[:, 48:120] = w_vp[...]
-    select = selection()
+    wv_s[0:48, :] = w_v[...]
+    wv_s[48:120, :] = w_vp[...]
     pat = tn(kfr[...], select, lax.Precision.HIGHEST)
     pat_s[...] = pat
     r64, l64 = iotas((LK, 128))
-    feat = nn(ks[...], wk_s[...])
+    feat = nt(ks[...], wk_s[...])
     k_rows = jnp.where(
         l64 < 48, feat, jnp.where(l64 < 84, rotated(feat, pat) + part(pat, 5), 0.0)
     ).astype(BF)
@@ -163,7 +179,7 @@
         k_full = jnp.where(
             l64 == at, high, jnp.where(l64 == at + 1, middle, jnp.where(l64 == at + 2, low, k_full))
         )
-    feat = nn(ks[...], wv_s[...])
+    feat = nt(ks[...], wv_s[...])
     v_rows = jnp.where(
         l64 < 48, feat, jnp.where(l64 < 120, rotated(feat, pat) + part(pat, 5), 0.0)
     ).astype(BF)
@@ -220,13 +236,18 @@
     for s in range(6):
         start_round(s, 0)
 
+    for load in loads[6:]:
+        load.wait()
     wq_s[...] = jnp.zeros_like(wq_s)
-    wq_s[:, 0:48] = w_q[...]
-    wq_s[:, 48:84] = w_qp[...]
-    pat_q = tn(qfr[...], select, lax.Precision.HIGHEST)
+    wq_s[0:48, :] = w_q[...]
+    wq_s[48:84, :] = w_qp[...]
+    pat_q = lax.dot_general(
+        qfr[...], select, (((1,), (0,)), ((), ())),
+        preferred_element_type=F32, precision=lax.Precision.HIGHEST,
+    )
     _, l1 = iotas((1, 128))
     x1 = l1 - 3 * third(l1)
-    feat = nn(qs[...], wq_s[...])
+    feat = nt(qs[...], wq_s[...])
     q_row = jnp.where(
         l1 < 48, feat, jnp.where(l1 < 84, rotated(feat, pat_q) + part(pat_q, 5), 0.0)
     )
@@ -392,7 +413,7 @@
     )
     d_q = jnp.sum(q_terms, axis=0, keepdims=True)
     d_q = jnp.where(l1 < 48, d_q, jnp.where(l1 < 84, unrotated(d_q, pat_q), 0.0)).astype(BF)
-    part_s[72:73, :] = nt(d_q, wq_s[...])
+    part_s[72:73, :] = nn(d_q, wq_s[...])
 
     own.wait()
     everyone = recv.at[pl.ds(0, ROWS - 1)]
@@ -431,7 +452,7 @@
     d_points = jnp.where(within(l64, 48, 36), gain_l * (out_k - sums * kf), 0.0)
     d_k = jnp.where(l64 < 48, out_k * 0.25, jnp.where(l64 < 84, unrotated(d_points, pat), 0.0))
     d_v = jnp.where(l64 < 48, out_v, jnp.where(l64 < 120, unrotated(out_v, pat), 0.0))
-    part_s[0:64, :] = nt(d_k.astype(BF), wk_s[...]) + nt(d_v.astype(BF), wv_s[...])
+    part_s[0:64, :] = nn(d_k.astype(BF), wk_s[...]) + nn(d_v.astype(BF), wv_s[...])
 
     exchange = pltpu.make_async_remote_copy(
         src_ref=part_s,
@@ -458,9 +479,7 @@
     w_query_points, w_key_points, w_value_points, head_weight, bias_weight, w_out, d_out,
 ):
     vmem = pl.BlockSpec(memory_space=pltpu.VMEM)
-    specs = [vmem] * 15
-    specs[2] = pl.BlockSpec(memory_space=pl.ANY)
-    specs[11] = pl.BlockSpec(memory_space=pltpu.SMEM)
+    specs = [pl.BlockSpec(memory_space=pltpu.HBM)] * 15
     dma = pltpu.SemaphoreType.DMA
     return pl.pallas_call(
         kernel,
@@ -472,12 +491,27 @@
         in_specs=specs,
         out_specs=(vmem, vmem, vmem),
         scratch_shapes=[
+            pltpu.VMEM((1, 384), BF),
+            pltpu.VMEM((LK, 384), BF),
+            pltpu.VMEM((1, 12), F32),
+            pltpu.VMEM((12, LK), F32),
+            pltpu.VMEM((48, 384), BF),
+            pltpu.VMEM((48, 384), BF),
+            pltpu.VMEM((48, 384), BF),
+            pltpu.VMEM((36, 384), BF),
+            pltpu.VMEM((36, 384), BF),
+            pltpu.VMEM((72, 384), BF),
+            pltpu.SMEM((3,), F32),
+            pltpu.VMEM((3, 128), BF),
+            pltpu.VMEM((528, 384), BF),
+            pltpu.VMEM((1, 384), BF),
+            pltpu.SemaphoreType.DMA((14,)),
             pltpu.VMEM((NY, NZ, NX, LK, 128), BF),
             pltpu.VMEM((NY, NZ, NX, LK, 128), BF),
             pltpu.VMEM((K, 128), BF),
-            pltpu.VMEM((384, 128), BF),
-            pltpu.VMEM((384, 128), BF),
-            pltpu.VMEM((384, 128), BF),
+            pltpu.VMEM((128, 384), BF),
+            pltpu.VMEM((128, 384), BF),
+            pltpu.VMEM((128, 384), BF),
             pltpu.VMEM((256, 384), BF),
             pltpu.VMEM((16, 128), F32),
             pltpu.VMEM((16, K), F32),
@@ -492,11 +526,11 @@
             dma, dma((6, ROUNDS, 2)), dma((6, ROUNDS, 2)), dma, dma, dma, dma, dma,
         ],
         compiler_params=pltpu.CompilerParams(
-            collective_id=0, has_side_effects=True, vmem_limit_bytes=48 * 1024 * 1024
+            collective_id=0, has_side_effects=True, vmem_limit_bytes=67043328
         ),
     )(
-        query_single, key_single, pair, query_frames, key_frames, w_query, w_key, w_value,
-        w_query_points, w_key_points, w_value_points, head_weight, bias_weight, w_out, d_out,
+        query_single, key_single, pair, query_frames.T, key_frames, w_query.T, w_key.T, w_value.T,
+        w_query_points.T, w_key_points.T, w_value_points.T, head_weight, bias_weight, w_out, d_out,
     )
 
 

time: 81 us -> 70.6 us (0.87)
  local copies, waits for them, and re-layouts: 14.6 us -> 4.02 us
    unnamed x26 -> x3, local copies, waits for them, and re-layouts: 14.6 us -> 4.02 us
where the time goes in v3:
time: 70.6 us; the launch traced here: 70.5 us
  Pallas kernels  65.8 us (93%)
  local copies, waits for them, and re-layouts  4.02 us (6%)
    pallas_call x1, Pallas kernels, shards(): pl.pallas_call(kernel, out_shape=(jax.ShapeDtypeStruct((1, 384), BF), jax...  65.8 us
    unnamed x3, local copies, waits for them, and re-layouts  4.02 us

profile of v3, /device:TPU:1, one launch (start us, length us, event | category | flops | bytes accessed | tf_op | source)
XLA Modules:
  0.0 70.5 jit_solution(10751488119592589718)
XLA Ops:
  0.6 65.8 %shard_map.166 = (bf16[1,384]{1,0:T(2,128)(2,1)}, f32[1,384]{1,0:T(1,128)}, f32[64,384]{1,0:T(8,128)}) custom-call(bf16[1,384]{1,0:T(2,128)(2,1)} %qs_h.1, bf16[64,384]{1,0:T(8,128)(2,1)} %ks_h.1, bf16[1,8192,128]{2,1,0:T(8,128)(2,1)} %pair.1, f32[1,12]{1,0:T(1,128)} %bitcast.13, f32[12,64]{1,0:T(8,128)} %kfr_h.1, bf16[48,384]{1,0:T(8,128)(2,1)} %bitcast.8, ...), custom_call_target="tpu_custom_call" | custom-call | tf_op jit(solution)/shard_map/pallas_call | solution.py:484
  66.4 1.2 %copy.21 = bf16[1,384]{1,0:T(2,128)(2,1)} copy(bf16[1,384]{1,0:T(2,128)(2,1)} %get-tuple-element.6) | data formatting | bytes 1536
  67.7 1.2 %copy.22 = f32[1,384]{1,0:T(1,128)} copy(f32[1,384]{1,0:T(1,128)} %get-tuple-element.7) | data formatting | bytes 3072
  68.9 1.5 %copy.23 = f32[64,384]{1,0:T(8,128)} copy(f32[64,384]{1,0:T(8,128)} %get-tuple-element.8) | data formatting | bytes 196608

commit v4 on v3

--- a/solution.py
+++ b/solution.py
@@ -19,14 +19,50 @@
 BF, F32 = jnp.bfloat16, jnp.float32
 
 STREAMS = (
-    (0, 0, 16, (2, 0, 1)),
-    (0, 16, 32, (0, 1, 2)),
-    (0, 48, 16, (1, 2, 0)),
-    (1, 0, 16, (2, 0, 1)),
-    (1, 16, 16, (0, 1, 2)),
-    (1, 32, 32, (1, 2, 0)),
+    (0, 0, 32, (0, 1, 2)),
+    (0, 32, 32, (2, 1, 0)),
+    (1, 0, 32, (0, 1, 2)),
+    (1, 32, 32, (2, 1, 0)),
 )
-ROUNDS = 8
+SLOTS = 7
+
+
+def gather_plan():
+    plan = []
+
+    def add(rnd, name, needs, axis, step, offsets, half=None):
+        plan.append((rnd, name, needs, axis, step, offsets, half))
+
+    for sign, mark in ((1, "+"), (-1, "-")):
+        add(0, "a" + mark, (), 0, sign, (0, 0, 0))
+    add(0, "b", (), 0, 2, (0, 0, 0))
+    first = ("a+", "a-", "b")
+    for k in range(NZ // 2):
+        for sign, mark in ((1, "+"), (-1, "-")):
+            needs = first if k == 0 else ("c%d%s" % (k - 1, mark),)
+            half = "blocks" if k == NZ // 2 - 1 else None
+            add(1 + k, "c%d%s" % (k, mark), needs, 1, sign, (None, -sign * k, 0), half)
+    for k in range(NZ // 2 + 1):
+        for side in (1, -1) if 0 < k < NZ // 2 else (1,):
+            offset = -side * k
+            if k == 0:
+                needs = first
+            elif k == NZ // 2:
+                needs = ("c%d+" % (k - 1), "c%d-" % (k - 1))
+            else:
+                needs = ("c%d%s" % (k - 1, "+" if side == 1 else "-"),)
+            for sign, mark in ((1, "+"), (-1, "-")):
+                name = "%d%s" % (offset, mark)
+                add(1 + k, "d" + name, needs, 2, sign, (None, offset, 0))
+                if k < NZ // 2:
+                    add(2 + k, "e" + name, ("d" + name,), 2, sign, (None, offset, -sign), "blocks")
+            if k == NZ // 2:
+                add(1 + k, "e%d" % offset, needs, 2, 2, (None, offset, 0))
+    return sorted(plan, key=lambda item: (item[0], item[1]))
+
+
+PLAN = gather_plan()
+NUMBER = {item[1]: n for n, item in enumerate(PLAN)}
 
 
 def nt(a, b):
@@ -113,11 +149,11 @@
 def kernel(
     qs_h, ks_h, pair, qfr_h, kfr_h, w_q_h, w_k_h, w_v_h, w_qp_h, w_kp_h, w_vp_h, hw_h, bw_h,
     w_o_h, d_o_h,
-    o_out, o_gq, o_gk,
+    o_sum,
     qs, ks, qfr, kfr, w_q, w_k, w_v, w_qp, w_kp, w_vp, hw, bw, w_o, d_o, in_sem,
-    buf_k, buf_v, pair_s, wq_s, wk_s, wv_s, wp_s, lhs_s, pb_s, att_s, da_s, msg, recv, recv_f,
+    buf_k, buf_v, pair_s, wq_s, wk_s, wv_s, wp_s, lhs_s, pb_s, att_s, da_s, msg_a, msg_s, recv_a, recv_s, unpack_a, unpack_s,
     pat_s, part_s, got_s,
-    pair_sem, send_sem, recv_sem, a2a_send, a2a_recv, own_sem, ex_send, ex_recv,
+    pair_sem, send_sem, recv_sem, a_send, a_recv, s_send, s_recv, own_sem, ex_send, ex_recv,
 ):
     row = lax.axis_index("row")
     core = lax.axis_index("head")
@@ -141,8 +177,8 @@
         return (moved[0] * NZ + moved[1]) * NX + moved[2]
 
     barrier = pltpu.get_barrier_semaphore()
-    for axis in range(3):
-        for step in (1, -1):
+    for axis, steps in ((0, (1, -1, 2)), (1, (1, -1)), (2, (1, -1, 2))):
+        for step in steps:
             pl.semaphore_signal(
                 barrier, inc=1, device_id=(neighbour(axis, step), core), device_id_type=MESH
             )
@@ -189,52 +225,55 @@
 
     bufs = (buf_k, buf_v)
 
-    def copies(s, rnd):
-        which, first, count, order = STREAMS[s]
-        left = rnd
-        for phase, axis in enumerate(order):
-            rounds = SIZES[axis] // 2
-            if left < rounds:
-                break
-            left -= rounds
-        out = []
-        for direction, step in enumerate((1, -1)):
-            at = [pl.ds(c, 1) for c in coords]
-            for done in order[:phase]:
-                at[done] = pl.ds(0, SIZES[done])
-            at[axis] = pl.ds((coords[axis] - step * left + SIZES[axis]) % SIZES[axis], 1)
-            if left == rounds - 1:
-                if phase == 0:
-                    if direction != s % 2:
-                        continue
-                else:
-                    split = order[0]
-                    at[split] = pl.ds(direction * (SIZES[split] // 2), SIZES[split] // 2)
-            where = bufs[which].at[at[0], at[1], at[2], pl.ds(first, count)]
-            out.append(
-                pltpu.make_async_remote_copy(
-                    src_ref=where,
-                    dst_ref=where,
-                    send_sem=send_sem.at[s, rnd, direction],
-                    recv_sem=recv_sem.at[s, rnd, direction],
-                    device_id=(neighbour(axis, step), core),
-                    device_id_type=MESH,
-                )
-            )
-        return out
-
-    pl.semaphore_wait(barrier, 7)
-
-    def start_round(s, rnd):
-        for copy in copies(s, rnd):
-            copy.start()
-
-    def end_round(s, rnd):
-        for copy in copies(s, rnd):
-            copy.wait_recv()
-
-    for s in range(6):
-        start_round(s, 0)
+    seen = [set() for _ in STREAMS]
+
+    def gather_copy(s, item):
+        which, start, count, order = STREAMS[s]
+        _, name, _, axis, step, offsets, half = item
+        at = [None] * 3
+        for a, offset in zip(order, offsets):
+            if offset is None:
+                at[a] = pl.ds(0, SIZES[a])
+            elif offset == 0:
+                at[a] = pl.ds(coords[a], 1)
+            else:
+                at[a] = pl.ds((coords[a] + offset + SIZES[a]) % SIZES[a], 1)
+        second = 0 if step == 1 else 1
+        if half == "blocks":
+            a = order[0]
+            at[a] = pl.ds(second * (SIZES[a] // 2), SIZES[a] // 2)
+        where = bufs[which].at[at[0], at[1], at[2], pl.ds(start, count)]
+        n = NUMBER[name]
+        return pltpu.make_async_remote_copy(
+            src_ref=where,
+            dst_ref=where,
+            send_sem=send_sem.at[s, n],
+            recv_sem=recv_sem.at[s, n],
+            device_id=(neighbour(order[axis], step), core),
+            device_id_type=MESH,
+        )
+
+    def arrive(s, name):
+        if name not in seen[s]:
+            seen[s].add(name)
+            gather_copy(s, PLAN[NUMBER[name]]).wait_recv()
+
+    def gather_round(s, rnd):
+        for item in PLAN:
+            if item[0] == rnd:
+                for name in item[2]:
+                    arrive(s, name)
+                gather_copy(s, item).start()
+        if rnd == SLOTS - 1:
+            for item in PLAN:
+                arrive(s, item[1])
+
+    def gather_slot(slot):
+        for s in range(4):
+            gather_round(s, slot)
+
+    pl.semaphore_wait(barrier, 9)
+    gather_slot(0)
 
     for load in loads[6:]:
         load.wait()
@@ -296,12 +335,10 @@
         pb_s[:, pl.ds(at, 1024)] = nt(lhs_p, pair_s[pl.ds(at, 1024), :])
         return 0
 
-    for rnd in range(1, ROUNDS + 1):
-        lax.fori_loop(rnd - 1, rnd, pair_step, 0)
-        for s in range(6):
-            end_round(s, rnd - 1)
-            if rnd < ROUNDS:
-                start_round(s, rnd)
+    for slot in range(1, SLOTS - 1):
+        lax.fori_loop((slot - 1) * 8 // (SLOTS - 2), slot * 8 // (SLOTS - 2), pair_step, 0)
+        gather_slot(slot)
+    gather_slot(SLOTS - 1)
 
     def chunk(ref, g):
         return ref[pl.ds(g // 2, 1), pl.ds((g % 2) * 4, 4)].reshape(1024, 128)
@@ -327,19 +364,61 @@
 
     total = lax.fori_loop(0, 8, exp_step, jnp.zeros((8, 1), F32))
 
-    def attend_step(g, carry):
+    rotate = row // 16
+    rc, _ = iotas((8, 1024))
+
+    def start_sends(message, landing, send, recv, g):
+        for n in range(16):
+            target = g * 16 + (row + n) % 16
+
+            def start(target=target):
+                at = pl.multiple_of((target // 2) * 128, 128)
+                pltpu.make_async_remote_copy(
+                    src_ref=message.at[:, pl.ds(at, 128)],
+                    dst_ref=landing.at[row],
+                    send_sem=send,
+                    recv_sem=recv,
+                    device_id=(target, core),
+                    device_id_type=MESH,
+                ).start()
+
+            if n:
+                start()
+            else:
+                pl.when(target != row)(start)
+
+    def own_copy(message, landing):
+        at = pl.multiple_of((row // 2) * 128, 128)
+        return pltpu.make_async_copy(message.at[:, pl.ds(at, 128)], landing.at[row], own_sem)
+
+    def all_of(landing, sem):
+        everyone = landing.at[pl.ds(0, ROWS - 1)]
+        return pltpu.make_async_copy(everyone, everyone, sem)
+
+    def attend_step(i, carry):
         acc_v, acc_p = carry
+        g = (i + rotate) % 8
+
+        @pl.when(i > 0)
+        def _():
+            start_sends(msg_a, recv_a, a_send, a_recv, (i - 1 + rotate) % 8)
+
         at = pl.multiple_of(g * 1024, 1024)
         a = att_s[:, pl.ds(at, 1024)] / total
         att_s[:, pl.ds(at, 1024)] = a
+        msg_a[:, pl.ds(at, 1024)] = jnp.where(rc < 3, a, side_k)[0:4].astype(BF)
         a = a.astype(BF)
         return (
             acc_v + nn(a, chunk(buf_v, g)),
             acc_p + nn(a, pair_s[pl.ds(at, 1024), :]),
         )
 
+    side_k = jnp.concatenate([q8] * 8, axis=1)
     zero8 = jnp.zeros((8, 128), F32)
     acc_v, acc_p = lax.fori_loop(0, 8, attend_step, (zero8, zero8))
+    start_sends(msg_a, recv_a, a_send, a_recv, (7 + rotate) % 8)
+    own_a = own_copy(msg_a, recv_a)
+    own_a.start()
     row_v = jnp.sum(jnp.where(values8, acc_v, 0.0), axis=0, keepdims=True)
     is_point = within(l1, 48, 72)
     local = jnp.where(is_point, unrotated(jnp.where(is_point, row_v - part(pat_q, 5), 0.0), pat_q), 0.0)
@@ -372,41 +451,29 @@
         return carry + jnp.sum(att_s[:, pl.ds(at, 1024)] * d_att, axis=1, keepdims=True)
 
     row_total = lax.fori_loop(0, 8, grad_step, jnp.zeros((8, 1), F32))
-    side = jnp.where(r8 == 6, q8, jnp.where(r8 == 7, side_v8, 0.0))
-    side = jnp.concatenate([side] * 8, axis=1)
-    rc, _ = iotas((8, 1024))
-
-    def score_step(g, carry):
+    side_v = jnp.concatenate([side_v8] * 8, axis=1)
+
+    def score_step(i, carry):
         acc, sums = carry
+        g = (i + rotate) % 8
+
+        @pl.when(i > 0)
+        def _():
+            start_sends(msg_s, recv_s, s_send, s_recv, (i - 1 + rotate) % 8)
+
         at = pl.multiple_of(g * 1024, 1024)
         a = att_s[:, pl.ds(at, 1024)]
         score = LOGIT_SCALE * a * (da_s[:, pl.ds(at, 1024)] - row_total)
-        out = jnp.where(rc < 3, a, jnp.where(rc < 6, pltpu.roll(score, 3, 0), side))
-        msg[:, pl.ds(at, 1024)] = out.astype(BF)
+        msg_s[:, pl.ds(at, 1024)] = jnp.where(rc < 3, score, side_v)[0:4].astype(BF)
         score = score.astype(BF)
         acc = acc + nn(score, chunk(buf_k, g))
         return acc, sums + jnp.sum(score.astype(F32), axis=1, keepdims=True)
 
     acc_k, score_rows = lax.fori_loop(0, 8, score_step, (zero8, jnp.zeros((8, 1), F32)))
-
-    def tile(device):
-        return msg.at[:, pl.ds(pl.multiple_of((device // 2) * 128, 128), 128)]
-
-    def send_step(i, _):
-        target = (row + i) % ROWS
-        pltpu.make_async_remote_copy(
-            src_ref=tile(target),
-            dst_ref=recv.at[row],
-            send_sem=a2a_send,
-            recv_sem=a2a_recv,
-            device_id=(target, core),
-            device_id_type=MESH,
-        ).start()
-        return 0
-
-    own = pltpu.make_async_copy(tile(row), recv.at[row], own_sem)
-    own.start()
-    lax.fori_loop(1, ROWS, send_step, 0)
+    start_sends(msg_s, recv_s, s_send, s_recv, (7 + rotate) % 8)
+    own_a.wait()
+    own_s = own_copy(msg_s, recv_s)
+    own_s.start()
 
     q_terms = jnp.where(keys8, acc_k * 0.25, 0.0) + jnp.where(
         points8, gain * (acc_k - score_rows * q8), 0.0
@@ -415,31 +482,33 @@
     d_q = jnp.where(l1 < 48, d_q, jnp.where(l1 < 84, unrotated(d_q, pat_q), 0.0)).astype(BF)
     part_s[72:73, :] = nn(d_q, wq_s[...])
 
-    own.wait()
-    everyone = recv.at[pl.ds(0, ROWS - 1)]
-    pltpu.make_async_copy(everyone, everyone, a2a_recv).wait()
-
-    def unpack_step(i, _):
-        at = pl.multiple_of(i * 64, 64)
-        recv_f[pl.ds(at, 64), :] = recv[pl.ds(i * 8, 8)].astype(F32).reshape(64, 128)
-        return 0
-
-    lax.fori_loop(0, ROWS // 8, unpack_step, 0)
-
-    def every(i):
-        return recv_f[pl.ds(i, ROWS, stride=8), :]
-
-    side_k, side_v = every(6), every(7)
     _, l128 = iotas((ROWS, 128))
+
+    def unpack(landing, unpacked):
+        def step(i, _):
+            at = pl.multiple_of(i * 32, 32)
+            unpacked[pl.ds(at, 32), :] = landing[pl.ds(i * 8, 8)].astype(F32).reshape(32, 128)
+            return 0
+
+        lax.fori_loop(0, ROWS // 8, step, 0)
+        return [unpacked[pl.ds(n, ROWS, stride=4), :] for n in range(4)]
+
+    all_of(recv_a, a_recv).wait()
+    *att_h, side_k = unpack(recv_a, unpack_a)
+    all_of(recv_s, s_recv).wait()
+    own_s.wait()
+    *score_h, side_v = unpack(recv_s, unpack_s)
     out_k = out_v = sums = jnp.zeros((128, 128), F32)
     for h in range(3):
         keys_h = within(l128, 16 * h, 16)
         points_h = within(l128, 48 + 12 * h, 12)
         vpoints_h = within(l128, 48 + 24 * h, 24)
-        att_h, score_h = every(h).astype(BF), every(3 + h).astype(BF)
-        out_v = out_v + tn(att_h, jnp.where(keys_h | vpoints_h, side_v, 0.0).astype(BF))
-        out_k = out_k + tn(score_h, jnp.where(keys_h | points_h, side_k, 0.0).astype(BF))
-        sums = sums + tn(score_h, jnp.where(points_h, 1.0, 0.0).astype(BF))
+        score = score_h[h].astype(BF)
+        out_v = out_v + tn(
+            att_h[h].astype(BF), jnp.where(keys_h | vpoints_h, side_v, 0.0).astype(BF)
+        )
+        out_k = out_k + tn(score, jnp.where(keys_h | points_h, side_k, 0.0).astype(BF))
+        sums = sums + tn(score, jnp.where(points_h, 1.0, 0.0).astype(BF))
     odd = row % 2 == 1
 
     def mine_of(x):
@@ -463,15 +532,19 @@
         device_id_type=MESH,
     )
     exchange.start()
-    for s in range(6):
-        for rnd in range(ROUNDS):
-            for copy in copies(s, rnd):
-                copy.wait_send()
-    pltpu.make_async_copy(everyone, everyone, a2a_send).wait()
+    for s in range(4):
+        for item in PLAN:
+            gather_copy(s, item).wait_send()
+    all_of(recv_a, a_send).wait()
+    all_of(recv_s, s_send).wait()
     exchange.wait()
-    o_gk[...] = part_s[0:64, :] + got_s[0:64, :]
-    o_out[...] = (part_s[64:65, :] + got_s[64:65, :]).astype(BF)
-    o_gq[...] = part_s[72:73, :] + got_s[72:73, :]
+    o_sum[...] = part_s[...] + got_s[...]
+
+
+def finish(total, o_out, o_gq, o_gk):
+    o_gk[...] = total[0:64, :]
+    o_out[...] = total[64:65, :].astype(BF)
+    o_gq[...] = total[72:73, :]
 
 
 def shards(
@@ -481,15 +554,11 @@
     vmem = pl.BlockSpec(memory_space=pltpu.VMEM)
     specs = [pl.BlockSpec(memory_space=pltpu.HBM)] * 15
     dma = pltpu.SemaphoreType.DMA
-    return pl.pallas_call(
+    total = pl.pallas_call(
         kernel,
-        out_shape=(
-            jax.ShapeDtypeStruct((1, 384), BF),
-            jax.ShapeDtypeStruct((1, 384), F32),
-            jax.ShapeDtypeStruct((LK, 384), F32),
-        ),
+        out_shape=jax.ShapeDtypeStruct((80, 384), F32),
         in_specs=specs,
-        out_specs=(vmem, vmem, vmem),
+        out_specs=vmem,
         scratch_shapes=[
             pltpu.VMEM((1, 384), BF),
             pltpu.VMEM((LK, 384), BF),
@@ -517,13 +586,16 @@
             pltpu.VMEM((16, K), F32),
             pltpu.VMEM((8, K), F32),
             pltpu.VMEM((8, K), F32),
-            pltpu.VMEM((8, K), BF),
-            pltpu.VMEM((ROWS, 8, 128), BF),
-            pltpu.VMEM((ROWS * 8, 128), F32),
+            pltpu.VMEM((4, K), BF),
+            pltpu.VMEM((4, K), BF),
+            pltpu.VMEM((ROWS, 4, 128), BF),
+            pltpu.VMEM((ROWS, 4, 128), BF),
+            pltpu.VMEM((ROWS * 4, 128), F32),
+            pltpu.VMEM((ROWS * 4, 128), F32),
             pltpu.VMEM((LK, 1280), F32),
             pltpu.VMEM((80, 384), F32),
             pltpu.VMEM((80, 384), F32),
-            dma, dma((6, ROUNDS, 2)), dma((6, ROUNDS, 2)), dma, dma, dma, dma, dma,
+            dma, dma((4, len(PLAN))), dma((4, len(PLAN))), dma, dma, dma, dma, dma, dma, dma,
         ],
         compiler_params=pltpu.CompilerParams(
             collective_id=0, has_side_effects=True, vmem_limit_bytes=67043328
@@ -532,6 +604,16 @@
         query_single, key_single, pair, query_frames.T, key_frames, w_query.T, w_key.T, w_value.T,
         w_query_points.T, w_key_points.T, w_value_points.T, head_weight, bias_weight, w_out, d_out,
     )
+    return pl.pallas_call(
+        finish,
+        out_shape=(
+            jax.ShapeDtypeStruct((1, 384), BF),
+            jax.ShapeDtypeStruct((1, 384), F32),
+            jax.ShapeDtypeStruct((LK, 384), F32),
+        ),
+        in_specs=[vmem],
+        out_specs=(vmem, vmem, vmem),
+    )(total)
 
 
 def solution(mesh):

time: 70.6 us -> 60 us (0.85)
  Pallas kernels: 65.8 us -> 59.3 us
  local copies, waits for them, and re-layouts: 4.02 us -> 0 us
    pallas_call x1 -> x2, Pallas kernels: 65.8 us -> 59.3 us  [the longest x1 57.7 us: shards(): pl.pallas_call(kernel, out_shape=jax.ShapeDtypeStruct((80, 384), F32), in...]
    unnamed x3 -> x0, local copies, waits for them, and re-layouts: 4.02 us -> none
where the time goes in v4:
time: 60 us; the launch traced here: 59.9 us
  Pallas kernels  59.3 us (99%)
  between operations  0.64 us (1%)
    pallas_call x1, Pallas kernels, shards(): pl.pallas_call(kernel, out_shape=jax.ShapeDtypeStruct((80, 384), F32), in...  57.7 us
    pallas_call x1, Pallas kernels, shards(): pl.pallas_call(finish, out_shape=(jax.ShapeDtypeStruct((1, 384), BF), jax...  1.55 us

profile of v4, /device:TPU:1, one launch (start us, length us, event | category | flops | bytes accessed | tf_op | source)
XLA Modules:
  0.0 59.9 jit_solution(18398020193716947535)
XLA Ops:
  0.6 57.7 %shard_map.166.total = f32[80,384]{1,0:T(8,128)} custom-call(bf16[1,384]{1,0:T(2,128)(2,1)} %qs_h.1, bf16[64,384]{1,0:T(8,128)(2,1)} %ks_h.1, bf16[1,8192,128]{2,1,0:T(8,128)(2,1)} %pair.1, f32[1,12]{1,0:T(1,128)} %bitcast.13, f32[12,64]{1,0:T(8,128)} %kfr_h.1, bf16[48,384]{1,0:T(8,128)(2,1)} %bitcast.8, bf16[48,384]{1,0:T(8,128)(2,1)} %bitcast.9, ...), custom_call_target="tpu_custom_call" | custom-call | tf_op jit(solution)/shard_map/pallas_call | solution.py:557
  58.3 1.6 %shard_map.167 = (bf16[1,384]{1,0:T(2,128)(2,1)}, f32[1,384]{1,0:T(1,128)}, f32[64,384]{1,0:T(8,128)}) custom-call(f32[80,384]{1,0:T(8,128)} %shard_map.166.total), custom_call_target="tpu_custom_call" | custom-call | tf_op jit(solution)/shard_map/pallas_call | solution.py:607

commit v5 on v4

--- a/solution.py
+++ b/solution.py
@@ -130,6 +130,13 @@
     return out
 
 
+def fold(x, combine):
+    parts = [x[:, 128 * n : 128 * n + 128] for n in range(x.shape[1] // 128)]
+    while len(parts) > 1:
+        parts = [combine(*parts[n : n + 2]) for n in range(0, len(parts), 2)]
+    return parts[0]
+
+
 def softplus(x):
     return jnp.maximum(x, 0.0) + jnp.log1p(jnp.exp(-jnp.abs(x)))
 
@@ -258,19 +265,20 @@
             seen[s].add(name)
             gather_copy(s, PLAN[NUMBER[name]]).wait_recv()
 
-    def gather_round(s, rnd):
+    def gather_round(s, rnd, last):
         for item in PLAN:
-            if item[0] == rnd:
+            if item[0] == rnd and (item[1][0] == "e") == last:
                 for name in item[2]:
                     arrive(s, name)
                 gather_copy(s, item).start()
-        if rnd == SLOTS - 1:
+        if rnd == SLOTS - 1 and last:
             for item in PLAN:
                 arrive(s, item[1])
 
     def gather_slot(slot):
-        for s in range(4):
-            gather_round(s, slot)
+        for last in (False, True):
+            for s in range(4):
+                gather_round(s, slot, last)
 
     pl.semaphore_wait(barrier, 9)
     gather_slot(0)
@@ -352,17 +360,20 @@
             + gain * (both[8:16] - 0.5 * q_square)
         )
         att_s[:, pl.ds(at, 1024)] = logits
-        return jnp.maximum(top, jnp.max(logits, axis=1, keepdims=True))
-
-    top = lax.fori_loop(0, 8, logit_step, jnp.full((8, 1), -3.0e38, F32))
+        return jnp.maximum(top, fold(logits, jnp.maximum))
+
+    top = lax.fori_loop(0, 8, logit_step, jnp.full((8, 128), -3.0e38, F32), unroll=8)
+    top = jnp.max(top, axis=1, keepdims=True)
 
     def exp_step(g, total):
         at = pl.multiple_of(g * 1024, 1024)
         e = jnp.exp(att_s[:, pl.ds(at, 1024)] - top)
         att_s[:, pl.ds(at, 1024)] = e
-        return total + jnp.sum(e, axis=1, keepdims=True)
-
-    total = lax.fori_loop(0, 8, exp_step, jnp.zeros((8, 1), F32))
+        return total + fold(e, jnp.add)
+
+    zero8 = jnp.zeros((8, 128), F32)
+    total = lax.fori_loop(0, 8, exp_step, zero8, unroll=8)
+    inverse = 1.0 / jnp.sum(total, axis=1, keepdims=True)
 
     rotate = row // 16
     rc, _ = iotas((8, 1024))
@@ -404,7 +415,7 @@
             start_sends(msg_a, recv_a, a_send, a_recv, (i - 1 + rotate) % 8)
 
         at = pl.multiple_of(g * 1024, 1024)
-        a = att_s[:, pl.ds(at, 1024)] / total
+        a = att_s[:, pl.ds(at, 1024)] * inverse
         att_s[:, pl.ds(at, 1024)] = a
         msg_a[:, pl.ds(at, 1024)] = jnp.where(rc < 3, a, side_k)[0:4].astype(BF)
         a = a.astype(BF)
@@ -414,8 +425,7 @@
         )
 
     side_k = jnp.concatenate([q8] * 8, axis=1)
-    zero8 = jnp.zeros((8, 128), F32)
-    acc_v, acc_p = lax.fori_loop(0, 8, attend_step, (zero8, zero8))
+    acc_v, acc_p = lax.fori_loop(0, 8, attend_step, (zero8, zero8), unroll=4)
     start_sends(msg_a, recv_a, a_send, a_recv, (7 + rotate) % 8)
     own_a = own_copy(msg_a, recv_a)
     own_a.start()
@@ -448,9 +458,10 @@
         at = pl.multiple_of(g * 1024, 1024)
         d_att = nt(lhs_v, chunk(buf_v, g)) + pb_s[8:16, pl.ds(at, 1024)]
         da_s[:, pl.ds(at, 1024)] = d_att
-        return carry + jnp.sum(att_s[:, pl.ds(at, 1024)] * d_att, axis=1, keepdims=True)
-
-    row_total = lax.fori_loop(0, 8, grad_step, jnp.zeros((8, 1), F32))
+        return carry + fold(att_s[:, pl.ds(at, 1024)] * d_att, jnp.add)
+
+    row_total = lax.fori_loop(0, 8, grad_step, zero8, unroll=8)
+    row_total = jnp.sum(row_total, axis=1, keepdims=True)
     side_v = jnp.concatenate([side_v8] * 8, axis=1)
 
     def score_step(i, carry):
@@ -467,9 +478,10 @@
         msg_s[:, pl.ds(at, 1024)] = jnp.where(rc < 3, score, side_v)[0:4].astype(BF)
         score = score.astype(BF)
         acc = acc + nn(score, chunk(buf_k, g))
-        return acc, sums + jnp.sum(score.astype(F32), axis=1, keepdims=True)
-
-    acc_k, score_rows = lax.fori_loop(0, 8, score_step, (zero8, jnp.zeros((8, 1), F32)))
+        return acc, sums + fold(score.astype(F32), jnp.add)
+
+    acc_k, score_rows = lax.fori_loop(0, 8, score_step, (zero8, zero8), unroll=4)
+    score_rows = jnp.sum(score_rows, axis=1, keepdims=True)
     start_sends(msg_s, recv_s, s_send, s_recv, (7 + rotate) % 8)
     own_a.wait()
     own_s = own_copy(msg_s, recv_s)
@@ -493,31 +505,37 @@
         lax.fori_loop(0, ROWS // 8, step, 0)
         return [unpacked[pl.ds(n, ROWS, stride=4), :] for n in range(4)]
 
+    odd = row % 2 == 1
+
+    def mine_of(x):
+        return jnp.where(odd, x[64:128], x[0:64])
+
+    for s in range(4):
+        for item in PLAN:
+            gather_copy(s, item).wait_send()
     all_of(recv_a, a_recv).wait()
     *att_h, side_k = unpack(recv_a, unpack_a)
+    keys_h = [within(l128, 16 * h, 16) for h in range(3)]
+    points_h = [within(l128, 48 + 12 * h, 12) for h in range(3)]
+    rights_k = [jnp.where(keys_h[h] | points_h[h], side_k, 0.0).astype(BF) for h in range(3)]
+    rights_n = [jnp.where(points_h[h], 1.0, 0.0).astype(BF) for h in range(3)]
+    pat = pat_s[...]
+    kf = buf_k[mine].reshape(LK, 128).astype(F32)
+    gain_l = softplus(by_head(jnp.where(l1 < 60, 0, jnp.where(l1 < 72, 1, 2)), raw)) * POINT_SCALE
+
     all_of(recv_s, s_recv).wait()
     own_s.wait()
     *score_h, side_v = unpack(recv_s, unpack_s)
     out_k = out_v = sums = jnp.zeros((128, 128), F32)
     for h in range(3):
-        keys_h = within(l128, 16 * h, 16)
-        points_h = within(l128, 48 + 12 * h, 12)
+        score = score_h[h].astype(BF)
         vpoints_h = within(l128, 48 + 24 * h, 24)
-        score = score_h[h].astype(BF)
         out_v = out_v + tn(
-            att_h[h].astype(BF), jnp.where(keys_h | vpoints_h, side_v, 0.0).astype(BF)
-        )
-        out_k = out_k + tn(score, jnp.where(keys_h | points_h, side_k, 0.0).astype(BF))
-        sums = sums + tn(score, jnp.where(points_h, 1.0, 0.0).astype(BF))
-    odd = row % 2 == 1
-
-    def mine_of(x):
-        return jnp.where(odd, x[64:128], x[0:64])
-
+            att_h[h].astype(BF), jnp.where(keys_h[h] | vpoints_h, side_v, 0.0).astype(BF)
+        )
+        out_k = out_k + tn(score, rights_k[h])
+        sums = sums + tn(score, rights_n[h])
     out_k, out_v, sums = mine_of(out_k), mine_of(out_v), mine_of(sums)
-    pat = pat_s[...]
-    kf = buf_k[mine].reshape(LK, 128).astype(F32)
-    gain_l = softplus(by_head(jnp.where(l1 < 60, 0, jnp.where(l1 < 72, 1, 2)), raw)) * POINT_SCALE
     d_points = jnp.where(within(l64, 48, 36), gain_l * (out_k - sums * kf), 0.0)
     d_k = jnp.where(l64 < 48, out_k * 0.25, jnp.where(l64 < 84, unrotated(d_points, pat), 0.0))
     d_v = jnp.where(l64 < 48, out_v, jnp.where(l64 < 120, unrotated(out_v, pat), 0.0))
@@ -532,9 +550,6 @@
         device_id_type=MESH,
     )
     exchange.start()
-    for s in range(4):
-        for item in PLAN:
-            gather_copy(s, item).wait_send()
     all_of(recv_a, a_send).wait()
     all_of(recv_s, s_send).wait()
     exchange.wait()
@@ -556,7 +571,7 @@
     dma = pltpu.SemaphoreType.DMA
     total = pl.pallas_call(
         kernel,
-        out_shape=jax.ShapeDtypeStruct((80, 384), F32),
+        out_shape=pltpu.VMEM((80, 384), F32),
         in_specs=specs,
         out_specs=vmem,
         scratch_shapes=[
@@ -598,7 +613,7 @@
             dma, dma((4, len(PLAN))), dma((4, len(PLAN))), dma, dma, dma, dma, dma, dma, dma,
         ],
         compiler_params=pltpu.CompilerParams(
-            collective_id=0, has_side_effects=True, vmem_limit_bytes=67043328
+            collective_id=0, has_side_effects=True, vmem_limit_bytes=66900000
         ),
     )(
         query_single, key_single, pair, query_frames.T, key_frames, w_query.T, w_key.T, w_value.T,
@@ -613,6 +628,7 @@
         ),
         in_specs=[vmem],
         out_specs=(vmem, vmem, vmem),
+        compiler_params=pltpu.CompilerParams(vmem_limit_bytes=16 * 1024 * 1024),
     )(total)
 
 

time: 60 us -> 53.9 us (0.90)
  Pallas kernels: 59.3 us -> 53.1 us
    pallas_call x1, Pallas kernels: 57.7 us -> 52.5 us  [shards(): pl.pallas_call(kernel, out_shape=pltpu.VMEM((80, 384), F32), in_specs=spe...]
    pallas_call x1, Pallas kernels: 1.55 us -> 0.66 us  [shards(): pl.pallas_call(finish, out_shape=(jax.ShapeDtypeStruct((1, 384), BF), jax...]
where the time goes in v5:
time: 53.9 us; the launch traced here: 53.8 us
  Pallas kernels  53.1 us (99%)
  between operations  0.64 us (1%)
    pallas_call x1, Pallas kernels, shards(): pl.pallas_call(kernel, out_shape=pltpu.VMEM((80, 384), F32), in_specs=spe...  52.5 us

profile of v5, /device:TPU:1, one launch (start us, length us, event | category | flops | bytes accessed | tf_op | source)
XLA Modules:
  0.0 53.8 jit_solution(12657501010640406506)
XLA Ops:
  0.6 52.5 %shard_map.166.total = f32[80,384]{1,0:T(8,128)S(1)} custom-call(bf16[1,384]{1,0:T(2,128)(2,1)} %qs_h.1, bf16[64,384]{1,0:T(8,128)(2,1)} %ks_h.1, bf16[1,8192,128]{2,1,0:T(8,128)(2,1)} %pair.1, f32[1,12]{1,0:T(1,128)} %bitcast.13, f32[12,64]{1,0:T(8,128)} %kfr_h.1, bf16[48,384]{1,0:T(8,128)(2,1)} %bitcast.8, bf16[48,384]{1,0:T(8,128)(2,1)} %bitcast.9, ...), custom_call_target="tpu_custom_call" | custom-call | tf_op jit(solution)/shard_map/pallas_call | solution.py:572
  53.1 0.7 %shard_map.167 = (bf16[1,384]{1,0:T(2,128)(2,1)}, f32[1,384]{1,0:T(1,128)}, f32[64,384]{1,0:T(8,128)}) custom-call(f32[80,384]{1,0:T(8,128)S(1)} %shard_map.166.total), custom_call_target="tpu_custom_call" | custom-call | tf_op jit(solution)/shard_map/pallas_call | solution.py:622

commit v6 on v5

--- a/solution.py
+++ b/solution.py
@@ -194,14 +194,11 @@
     pair_copy.start()
 
     select = selection()
-    for load in loads[:6]:
+    for load in loads[:4]:
         load.wait()
     wk_s[...] = jnp.zeros_like(wk_s)
     wk_s[0:48, :] = w_k[...]
     wk_s[48:84, :] = w_kp[...]
-    wv_s[...] = jnp.zeros_like(wv_s)
-    wv_s[0:48, :] = w_v[...]
-    wv_s[48:120, :] = w_vp[...]
     pat = tn(kfr[...], select, lax.Precision.HIGHEST)
     pat_s[...] = pat
     r64, l64 = iotas((LK, 128))
@@ -222,13 +219,8 @@
         k_full = jnp.where(
             l64 == at, high, jnp.where(l64 == at + 1, middle, jnp.where(l64 == at + 2, low, k_full))
         )
-    feat = nt(ks[...], wv_s[...])
-    v_rows = jnp.where(
-        l64 < 48, feat, jnp.where(l64 < 120, rotated(feat, pat) + part(pat, 5), 0.0)
-    ).astype(BF)
     mine = (pl.ds(coords[0], 1), pl.ds(coords[1], 1), pl.ds(coords[2], 1))
     buf_k[mine] = k_full.astype(BF).reshape(1, 1, 1, LK, 128)
-    buf_v[mine] = v_rows.reshape(1, 1, 1, LK, 128)
 
     bufs = (buf_k, buf_v)
 
@@ -275,13 +267,24 @@
             for item in PLAN:
                 arrive(s, item[1])
 
-    def gather_slot(slot):
+    def gather_slot(slot, streams=range(4)):
         for last in (False, True):
-            for s in range(4):
+            for s in streams:
                 gather_round(s, slot, last)
 
     pl.semaphore_wait(barrier, 9)
-    gather_slot(0)
+    gather_slot(0, (0, 1))
+    for load in loads[4:6]:
+        load.wait()
+    wv_s[...] = jnp.zeros_like(wv_s)
+    wv_s[0:48, :] = w_v[...]
+    wv_s[48:120, :] = w_vp[...]
+    feat = nt(ks[...], wv_s[...])
+    v_rows = jnp.where(
+        l64 < 48, feat, jnp.where(l64 < 120, rotated(feat, pat) + part(pat, 5), 0.0)
+    ).astype(BF)
+    buf_v[mine] = v_rows.reshape(1, 1, 1, LK, 128)
+    gather_slot(0, (2, 3))
 
     for load in loads[6:]:
         load.wait()
@@ -314,6 +317,7 @@
         axis=0,
     ).astype(BF)
 
+    gather_slot(1)
     i256, _ = iotas((256, 1))
     i = i256 & 127
     j = i - 48
@@ -343,10 +347,10 @@
         pb_s[:, pl.ds(at, 1024)] = nt(lhs_p, pair_s[pl.ds(at, 1024), :])
         return 0
 
-    for slot in range(1, SLOTS - 1):
-        lax.fori_loop((slot - 1) * 8 // (SLOTS - 2), slot * 8 // (SLOTS - 2), pair_step, 0)
+    for slot in range(2, SLOTS - 1):
+        lax.fori_loop((slot - 2) * 2, (slot - 1) * 2, pair_step, 0)
         gather_slot(slot)
-    gather_slot(SLOTS - 1)
+    gather_slot(SLOTS - 1, (0, 1))
 
     def chunk(ref, g):
         return ref[pl.ds(g // 2, 1), pl.ds((g % 2) * 4, 4)].reshape(1024, 128)
@@ -373,6 +377,7 @@
 
     zero8 = jnp.zeros((8, 128), F32)
     total = lax.fori_loop(0, 8, exp_step, zero8, unroll=8)
+    gather_slot(SLOTS - 1, (2, 3))
     inverse = 1.0 / jnp.sum(total, axis=1, keepdims=True)
 
     rotate = row // 16
@@ -406,8 +411,7 @@
         everyone = landing.at[pl.ds(0, ROWS - 1)]
         return pltpu.make_async_copy(everyone, everyone, sem)
 
-    def attend_step(i, carry):
-        acc_v, acc_p = carry
+    def attend_step(i, acc_v):
         g = (i + rotate) % 8
 
         @pl.when(i > 0)
@@ -418,14 +422,10 @@
         a = att_s[:, pl.ds(at, 1024)] * inverse
         att_s[:, pl.ds(at, 1024)] = a
         msg_a[:, pl.ds(at, 1024)] = jnp.where(rc < 3, a, side_k)[0:4].astype(BF)
-        a = a.astype(BF)
-        return (
-            acc_v + nn(a, chunk(buf_v, g)),
-            acc_p + nn(a, pair_s[pl.ds(at, 1024), :]),
-        )
+        return acc_v + nn(a.astype(BF), chunk(buf_v, g))
 
     side_k = jnp.concatenate([q8] * 8, axis=1)
-    acc_v, acc_p = lax.fori_loop(0, 8, attend_step, (zero8, zero8), unroll=4)
+    acc_v = lax.fori_loop(0, 8, attend_step, zero8, unroll=4)
     start_sends(msg_a, recv_a, a_send, a_recv, (7 + rotate) % 8)
     own_a = own_copy(msg_a, recv_a)
     own_a.start()
@@ -437,6 +437,55 @@
     for d in SHIFTS[1:]:
         norm = norm + jnp.where((x1 + d >= 0) & (x1 + d < 3), shifted(squares, d), 0.0)
     lengths = jnp.sqrt(1.0 + norm)
+    d_local = d_feat[:, 0:128] + d_feat[:, 128:256] / lengths * local
+    d_local = jnp.where(is_point, d_local, 0.0)
+    side_v = jnp.where(
+        l1 < 48, d_feat[:, 0:128], jnp.where(is_point, rotated(d_local, pat_q), 0.0)
+    )
+    side_v8 = jnp.broadcast_to(side_v, (8, 128))
+    lhs_v = jnp.where(values8, side_v8, 0.0).astype(BF)
+
+    def grad_step(g, carry):
+        at = pl.multiple_of(g * 1024, 1024)
+        d_att = nt(lhs_v, chunk(buf_v, g)) + pb_s[8:16, pl.ds(at, 1024)]
+        da_s[:, pl.ds(at, 1024)] = d_att
+        return carry + fold(att_s[:, pl.ds(at, 1024)] * d_att, jnp.add)
+
+    row_total = lax.fori_loop(0, 8, grad_step, zero8, unroll=8)
+    row_total = jnp.sum(row_total, axis=1, keepdims=True)
+    side_v = jnp.concatenate([side_v8] * 8, axis=1)
+
+    def score_step(i, sums):
+        g = (i + rotate) % 8
+
+        @pl.when(i > 0)
+        def _():
+            start_sends(msg_s, recv_s, s_send, s_recv, (i - 1 + rotate) % 8)
+
+        at = pl.multiple_of(g * 1024, 1024)
+        a = att_s[:, pl.ds(at, 1024)]
+        score = LOGIT_SCALE * a * (da_s[:, pl.ds(at, 1024)] - row_total)
+        msg_s[:, pl.ds(at, 1024)] = jnp.where(rc < 3, score, side_v)[0:4].astype(BF)
+        score = score.astype(BF).astype(F32)
+        da_s[:, pl.ds(at, 1024)] = score
+        return sums + fold(score, jnp.add)
+
+    score_rows = lax.fori_loop(0, 8, score_step, zero8, unroll=4)
+    score_rows = jnp.sum(score_rows, axis=1, keepdims=True)
+    start_sends(msg_s, recv_s, s_send, s_recv, (7 + rotate) % 8)
+    own_a.wait()
+    own_s = own_copy(msg_s, recv_s)
+    own_s.start()
+
+    def rest_step(g, carry):
+        acc_k, acc_p = carry
+        at = pl.multiple_of(g * 1024, 1024)
+        return (
+            acc_k + nn(da_s[:, pl.ds(at, 1024)].astype(BF), chunk(buf_k, g)),
+            acc_p + nn(att_s[:, pl.ds(at, 1024)].astype(BF), pair_s[pl.ds(at, 1024), :]),
+        )
+
+    acc_k, acc_p = lax.fori_loop(0, 8, rest_step, (zero8, zero8), unroll=4)
     f_v = jnp.where(l1 < 48, row_v, local).astype(BF)
     f_len = jnp.where(is_point & (x1 == 0), lengths, 0.0).astype(BF)
     out_row = nn(f_v, wp_s[0:128, :]) + nn(f_len, wp_s[128:256, :])
@@ -446,47 +495,6 @@
         )
     part_s[64:65, :] = out_row
 
-    d_local = d_feat[:, 0:128] + d_feat[:, 128:256] / lengths * local
-    d_local = jnp.where(is_point, d_local, 0.0)
-    side_v = jnp.where(
-        l1 < 48, d_feat[:, 0:128], jnp.where(is_point, rotated(d_local, pat_q), 0.0)
-    )
-    side_v8 = jnp.broadcast_to(side_v, (8, 128))
-    lhs_v = jnp.where(values8, side_v8, 0.0).astype(BF)
-
-    def grad_step(g, carry):
-        at = pl.multiple_of(g * 1024, 1024)
-        d_att = nt(lhs_v, chunk(buf_v, g)) + pb_s[8:16, pl.ds(at, 1024)]
-        da_s[:, pl.ds(at, 1024)] = d_att
-        return carry + fold(att_s[:, pl.ds(at, 1024)] * d_att, jnp.add)
-
-    row_total = lax.fori_loop(0, 8, grad_step, zero8, unroll=8)
-    row_total = jnp.sum(row_total, axis=1, keepdims=True)
-    side_v = jnp.concatenate([side_v8] * 8, axis=1)
-
-    def score_step(i, carry):
-        acc, sums = carry
-        g = (i + rotate) % 8
-
-        @pl.when(i > 0)
-        def _():
-            start_sends(msg_s, recv_s, s_send, s_recv, (i - 1 + rotate) % 8)
-
-        at = pl.multiple_of(g * 1024, 1024)
-        a = att_s[:, pl.ds(at, 1024)]
-        score = LOGIT_SCALE * a * (da_s[:, pl.ds(at, 1024)] - row_total)
-        msg_s[:, pl.ds(at, 1024)] = jnp.where(rc < 3, score, side_v)[0:4].astype(BF)
-        score = score.astype(BF)
-        acc = acc + nn(score, chunk(buf_k, g))
-        return acc, sums + fold(score.astype(F32), jnp.add)
-
-    acc_k, score_rows = lax.fori_loop(0, 8, score_step, (zero8, zero8), unroll=4)
-    score_rows = jnp.sum(score_rows, axis=1, keepdims=True)
-    start_sends(msg_s, recv_s, s_send, s_recv, (7 + rotate) % 8)
-    own_a.wait()
-    own_s = own_copy(msg_s, recv_s)
-    own_s.start()
-
     q_terms = jnp.where(keys8, acc_k * 0.25, 0.0) + jnp.where(
         points8, gain * (acc_k - score_rows * q8), 0.0
     )
@@ -502,7 +510,7 @@
             unpacked[pl.ds(at, 32), :] = landing[pl.ds(i * 8, 8)].astype(F32).reshape(32, 128)
             return 0
 
-        lax.fori_loop(0, ROWS // 8, step, 0)
+        lax.fori_loop(0, ROWS // 8, step, 0, unroll=4)
         return [unpacked[pl.ds(n, ROWS, stride=4), :] for n in range(4)]
 
     odd = row % 2 == 1

time: 53.9 us -> 52.2 us (0.968)
  Pallas kernels: 53.1 us -> 51.4 us
    pallas_call x1, Pallas kernels: 52.5 us -> 50.8 us  [shards(): pl.pallas_call(kernel, out_shape=pltpu.VMEM((80, 384), F32), in_specs=spe...]
where the time goes in v6:
time: 52.2 us; the launch traced here: 52.1 us
  Pallas kernels  51.4 us (98%)
  between operations  0.64 us (1%)
    pallas_call x1, Pallas kernels, shards(): pl.pallas_call(kernel, out_shape=pltpu.VMEM((80, 384), F32), in_specs=spe...  50.8 us

profile of v6, /device:TPU:1, one launch (start us, length us, event | category | flops | bytes accessed | tf_op | source)
XLA Modules:
  0.0 52.1 jit_solution(10729522208347062641)
XLA Ops:
  0.6 50.8 %shard_map.166.total = f32[80,384]{1,0:T(8,128)S(1)} custom-call(bf16[1,384]{1,0:T(2,128)(2,1)} %qs_h.1, bf16[64,384]{1,0:T(8,128)(2,1)} %ks_h.1, bf16[1,8192,128]{2,1,0:T(8,128)(2,1)} %pair.1, f32[1,12]{1,0:T(1,128)} %bitcast.13, f32[12,64]{1,0:T(8,128)} %kfr_h.1, bf16[48,384]{1,0:T(8,128)(2,1)} %bitcast.8, bf16[48,384]{1,0:T(8,128)(2,1)} %bitcast.9, ...), custom_call_target="tpu_custom_call" | custom-call | tf_op jit(solution)/shard_map/pallas_call | solution.py:580
  51.4 0.7 %shard_map.167 = (bf16[1,384]{1,0:T(2,128)(2,1)}, f32[1,384]{1,0:T(1,128)}, f32[64,384]{1,0:T(8,128)}) custom-call(f32[80,384]{1,0:T(8,128)S(1)} %shard_map.166.total), custom_call_target="tpu_custom_call" | custom-call | tf_op jit(solution)/shard_map/pallas_call | solution.py:630

commit v7 on v6

--- a/solution.py
+++ b/solution.py
@@ -176,11 +176,19 @@
     ]
     for load in loads:
         load.start()
-    coords = (row // (NZ * NX), (row // NX) % NZ, row % NX)
+    coords = (lax.div(row, NZ * NX), lax.rem(lax.div(row, NX), NZ), lax.rem(row, NX))
+    places = {}
+
+    def place(axis, offset):
+        if offset == 0:
+            return coords[axis]
+        if (axis, offset) not in places:
+            places[axis, offset] = lax.rem(coords[axis] + offset + SIZES[axis], SIZES[axis])
+        return places[axis, offset]
 
     def neighbour(axis, step):
         moved = list(coords)
-        moved[axis] = (coords[axis] + step + SIZES[axis]) % SIZES[axis]
+        moved[axis] = place(axis, step)
         return (moved[0] * NZ + moved[1]) * NX + moved[2]
 
     barrier = pltpu.get_barrier_semaphore()
@@ -233,10 +241,8 @@
         for a, offset in zip(order, offsets):
             if offset is None:
                 at[a] = pl.ds(0, SIZES[a])
-            elif offset == 0:
-                at[a] = pl.ds(coords[a], 1)
             else:
-                at[a] = pl.ds((coords[a] + offset + SIZES[a]) % SIZES[a], 1)
+                at[a] = pl.ds(place(a, offset), 1)
         second = 0 if step == 1 else 1
         if half == "blocks":
             a = order[0]
@@ -353,7 +359,7 @@
     gather_slot(SLOTS - 1, (0, 1))
 
     def chunk(ref, g):
-        return ref[pl.ds(g // 2, 1), pl.ds((g % 2) * 4, 4)].reshape(1024, 128)
+        return ref[pl.ds(lax.div(g, 2), 1), pl.ds(lax.rem(g, 2) * 4, 4)].reshape(1024, 128)
 
     def logit_step(g, top):
         at = pl.multiple_of(g * 1024, 1024)
@@ -380,31 +386,29 @@
     gather_slot(SLOTS - 1, (2, 3))
     inverse = 1.0 / jnp.sum(total, axis=1, keepdims=True)
 
-    rotate = row // 16
+    rotate = lax.div(row, 16)
+    inner = [lax.rem(row + n, 16) for n in range(16)]
+    pairs = [lax.div(n, 2) * 128 for n in inner]
     rc, _ = iotas((8, 1024))
 
-    def start_sends(message, landing, send, recv, g):
-        for n in range(16):
-            target = g * 16 + (row + n) % 16
-
-            def start(target=target):
-                at = pl.multiple_of((target // 2) * 128, 128)
-                pltpu.make_async_remote_copy(
-                    src_ref=message.at[:, pl.ds(at, 128)],
-                    dst_ref=landing.at[row],
-                    send_sem=send,
-                    recv_sem=recv,
-                    device_id=(target, core),
-                    device_id_type=MESH,
-                ).start()
-
-            if n:
-                start()
-            else:
-                pl.when(target != row)(start)
+    def group(i):
+        return lax.rem(i + rotate, 8)
+
+    def start_sends(message, landing, send, recv, i):
+        g = group(i)
+        for n in range(1 if i == 0 else 0, 16):
+            at = pl.multiple_of(g * 1024 + pairs[n], 128)
+            pltpu.make_async_remote_copy(
+                src_ref=message.at[:, pl.ds(at, 128)],
+                dst_ref=landing.at[row],
+                send_sem=send,
+                recv_sem=recv,
+                device_id=(g * 16 + inner[n], core),
+                device_id_type=MESH,
+            ).start()
 
     def own_copy(message, landing):
-        at = pl.multiple_of((row // 2) * 128, 128)
+        at = pl.multiple_of(lax.div(row, 2) * 128, 128)
         return pltpu.make_async_copy(message.at[:, pl.ds(at, 128)], landing.at[row], own_sem)
 
     def all_of(landing, sem):
@@ -412,11 +416,9 @@
         return pltpu.make_async_copy(everyone, everyone, sem)
 
     def attend_step(i, acc_v):
-        g = (i + rotate) % 8
-
-        @pl.when(i > 0)
-        def _():
-            start_sends(msg_a, recv_a, a_send, a_recv, (i - 1 + rotate) % 8)
+        g = group(i)
+        if i:
+            start_sends(msg_a, recv_a, a_send, a_recv, i - 1)
 
         at = pl.multiple_of(g * 1024, 1024)
         a = att_s[:, pl.ds(at, 1024)] * inverse
@@ -425,8 +427,10 @@
         return acc_v + nn(a.astype(BF), chunk(buf_v, g))
 
     side_k = jnp.concatenate([q8] * 8, axis=1)
-    acc_v = lax.fori_loop(0, 8, attend_step, zero8, unroll=4)
-    start_sends(msg_a, recv_a, a_send, a_recv, (7 + rotate) % 8)
+    acc_v = zero8
+    for i in range(8):
+        acc_v = attend_step(i, acc_v)
+    start_sends(msg_a, recv_a, a_send, a_recv, 7)
     own_a = own_copy(msg_a, recv_a)
     own_a.start()
     row_v = jnp.sum(jnp.where(values8, acc_v, 0.0), axis=0, keepdims=True)
@@ -456,11 +460,9 @@
     side_v = jnp.concatenate([side_v8] * 8, axis=1)
 
     def score_step(i, sums):
-        g = (i + rotate) % 8
-
-        @pl.when(i > 0)
-        def _():
-            start_sends(msg_s, recv_s, s_send, s_recv, (i - 1 + rotate) % 8)
+        g = group(i)
+        if i:
+            start_sends(msg_s, recv_s, s_send, s_recv, i - 1)
 
         at = pl.multiple_of(g * 1024, 1024)
         a = att_s[:, pl.ds(at, 1024)]
@@ -470,9 +472,11 @@
         da_s[:, pl.ds(at, 1024)] = score
         return sums + fold(score, jnp.add)
 
-    score_rows = lax.fori_loop(0, 8, score_step, zero8, unroll=4)
+    score_rows = zero8
+    for i in range(8):
+        score_rows = score_step(i, score_rows)
     score_rows = jnp.sum(score_rows, axis=1, keepdims=True)
-    start_sends(msg_s, recv_s, s_send, s_recv, (7 + rotate) % 8)
+    start_sends(msg_s, recv_s, s_send, s_recv, 7)
     own_a.wait()
     own_s = own_copy(msg_s, recv_s)
     own_s.start()
@@ -513,7 +517,7 @@
         lax.fori_loop(0, ROWS // 8, step, 0, unroll=4)
         return [unpacked[pl.ds(n, ROWS, stride=4), :] for n in range(4)]
 
-    odd = row % 2 == 1
+    odd = lax.rem(row, 2) == 1
 
     def mine_of(x):
         return jnp.where(odd, x[64:128], x[0:64])
@@ -525,8 +529,16 @@
     *att_h, side_k = unpack(recv_a, unpack_a)
     keys_h = [within(l128, 16 * h, 16) for h in range(3)]
     points_h = [within(l128, 48 + 12 * h, 12) for h in range(3)]
-    rights_k = [jnp.where(keys_h[h] | points_h[h], side_k, 0.0).astype(BF) for h in range(3)]
-    rights_n = [jnp.where(points_h[h], 1.0, 0.0).astype(BF) for h in range(3)]
+    rights = [
+        jnp.concatenate(
+            [
+                jnp.where(keys_h[h] | points_h[h], side_k, 0.0).astype(BF),
+                jnp.where(points_h[h], 1.0, 0.0).astype(BF),
+            ],
+            axis=1,
+        )
+        for h in range(3)
+    ]
     pat = pat_s[...]
     kf = buf_k[mine].reshape(LK, 128).astype(F32)
     gain_l = softplus(by_head(jnp.where(l1 < 60, 0, jnp.where(l1 < 72, 1, 2)), raw)) * POINT_SCALE
@@ -534,16 +546,17 @@
     all_of(recv_s, s_recv).wait()
     own_s.wait()
     *score_h, side_v = unpack(recv_s, unpack_s)
-    out_k = out_v = sums = jnp.zeros((128, 128), F32)
+    out_v = jnp.zeros((128, 128), F32)
+    both = jnp.zeros((128, 256), F32)
     for h in range(3):
         score = score_h[h].astype(BF)
         vpoints_h = within(l128, 48 + 24 * h, 24)
         out_v = out_v + tn(
             att_h[h].astype(BF), jnp.where(keys_h[h] | vpoints_h, side_v, 0.0).astype(BF)
         )
-        out_k = out_k + tn(score, rights_k[h])
-        sums = sums + tn(score, rights_n[h])
-    out_k, out_v, sums = mine_of(out_k), mine_of(out_v), mine_of(sums)
+        both = both + tn(score, rights[h])
+    out_v, both = mine_of(out_v), mine_of(both)
+    out_k, sums = both[:, 0:128], both[:, 128:256]
     d_points = jnp.where(within(l64, 48, 36), gain_l * (out_k - sums * kf), 0.0)
     d_k = jnp.where(l64 < 48, out_k * 0.25, jnp.where(l64 < 84, unrotated(d_points, pat), 0.0))
     d_v = jnp.where(l64 < 48, out_v, jnp.where(l64 < 120, unrotated(out_v, pat), 0.0))

time: 52.2 us -> 50.9 us (0.975)
  Pallas kernels: 51.4 us -> 50.2 us
    pallas_call x1, Pallas kernels: 50.8 us -> 49.5 us  [shards(): pl.pallas_call(kernel, out_shape=pltpu.VMEM((80, 384), F32), in_specs=spe...]
where the time goes in v7:
time: 50.9 us; the launch traced here: 50.8 us
  Pallas kernels  50.2 us (99%)
  between operations  0.64 us (1%)
    pallas_call x1, Pallas kernels, shards(): pl.pallas_call(kernel, out_shape=pltpu.VMEM((80, 384), F32), in_specs=spe...  49.5 us

profile of v7, /device:TPU:1, one launch (start us, length us, event | category | flops | bytes accessed | tf_op | source)
XLA Modules:
  0.0 50.8 jit_solution(3825172102491068928)
XLA Ops:
  0.6 49.5 %shard_map.166.total = f32[80,384]{1,0:T(8,128)S(1)} custom-call(bf16[1,384]{1,0:T(2,128)(2,1)} %qs_h.1, bf16[64,384]{1,0:T(8,128)(2,1)} %ks_h.1, bf16[1,8192,128]{2,1,0:T(8,128)(2,1)} %pair.1, f32[1,12]{1,0:T(1,128)} %bitcast.13, f32[12,64]{1,0:T(8,128)} %kfr_h.1, bf16[48,384]{1,0:T(8,128)(2,1)} %bitcast.8, bf16[48,384]{1,0:T(8,128)(2,1)} %bitcast.9, ...), custom_call_target="tpu_custom_call" | custom-call | tf_op jit(solution)/shard_map/pallas_call | solution.py:593
  50.2 0.7 %shard_map.167 = (bf16[1,384]{1,0:T(2,128)(2,1)}, f32[1,384]{1,0:T(1,128)}, f32[64,384]{1,0:T(8,128)}) custom-call(f32[80,384]{1,0:T(8,128)S(1)} %shard_map.166.total), custom_call_target="tpu_custom_call" | custom-call | tf_op jit(solution)/shard_map/pallas_call | solution.py:643

commit v8 on v7

--- a/solution.py
+++ b/solution.py
@@ -105,10 +105,13 @@
         ok = (x + d >= 0) & (x + d < 3)
         parts.append(ok & (j == 4 * x + d))
     parts.append(j == 9 + x)
+    back = []
     for d in SHIFTS[1:]:
         ok = (x + d >= 0) & (x + d < 3)
-        parts.append(ok & (j == 4 * x + 3 * d))
-    return jnp.concatenate([jnp.where(p, 1.0, 0.0) for p in parts], axis=1)
+        back.append(ok & (j == 4 * x + 3 * d))
+    return tuple(
+        jnp.concatenate([jnp.where(p, 1.0, 0.0) for p in group], axis=1) for group in (parts, back)
+    )
 
 
 def part(pat, i):
@@ -201,14 +204,14 @@
     pair_copy = pltpu.make_async_copy(pair.at[0], pair_s, pair_sem)
     pair_copy.start()
 
-    select = selection()
+    select, select_back = selection()
     for load in loads[:4]:
         load.wait()
     wk_s[...] = jnp.zeros_like(wk_s)
     wk_s[0:48, :] = w_k[...]
     wk_s[48:84, :] = w_kp[...]
     pat = tn(kfr[...], select, lax.Precision.HIGHEST)
-    pat_s[...] = pat
+    pat_s[:, 0:768] = pat
     r64, l64 = iotas((LK, 128))
     feat = nt(ks[...], wk_s[...])
     k_rows = jnp.where(
@@ -291,6 +294,7 @@
     ).astype(BF)
     buf_v[mine] = v_rows.reshape(1, 1, 1, LK, 128)
     gather_slot(0, (2, 3))
+    pat_s[:, 768:1280] = tn(kfr[...], select_back, lax.Precision.HIGHEST)
 
     for load in loads[6:]:
         load.wait()
@@ -298,7 +302,7 @@
     wq_s[0:48, :] = w_q[...]
     wq_s[48:84, :] = w_qp[...]
     pat_q = lax.dot_general(
-        qfr[...], select, (((1,), (0,)), ((), ())),
+        qfr[...], jnp.concatenate([select, select_back], axis=1), (((1,), (0,)), ((), ())),
         preferred_element_type=F32, precision=lax.Precision.HIGHEST,
     )
     _, l1 = iotas((1, 128))
@@ -514,7 +518,7 @@
             unpacked[pl.ds(at, 32), :] = landing[pl.ds(i * 8, 8)].astype(F32).reshape(32, 128)
             return 0
 
-        lax.fori_loop(0, ROWS // 8, step, 0, unroll=4)
+        lax.fori_loop(0, ROWS // 8, step, 0, unroll=16)
         return [unpacked[pl.ds(n, ROWS, stride=4), :] for n in range(4)]
 
     odd = lax.rem(row, 2) == 1

time: 50.9 us -> 50.9 us (level)
  no operation moved by 1% of the time
where the time goes in v8:
time: 50.9 us; the launch traced here: 50.8 us
  Pallas kernels  50.1 us (98%)
  between operations  0.64 us (1%)
    pallas_call x1, Pallas kernels, shards(): pl.pallas_call(kernel, out_shape=pltpu.VMEM((80, 384), F32), in_specs=spe...  49.5 us

profile of v8, /device:TPU:1, one launch (start us, length us, event | category | flops | bytes accessed | tf_op | source)
XLA Modules:
  0.0 50.8 jit_solution(7063853288129677136)
XLA Ops:
  0.6 49.5 %shard_map.166.total = f32[80,384]{1,0:T(8,128)S(1)} custom-call(bf16[1,384]{1,0:T(2,128)(2,1)} %qs_h.1, bf16[64,384]{1,0:T(8,128)(2,1)} %ks_h.1, bf16[1,8192,128]{2,1,0:T(8,128)(2,1)} %pair.1, f32[1,12]{1,0:T(1,128)} %bitcast.13, f32[12,64]{1,0:T(8,128)} %kfr_h.1, bf16[48,384]{1,0:T(8,128)(2,1)} %bitcast.8, bf16[48,384]{1,0:T(8,128)(2,1)} %bitcast.9, ...), custom_call_target="tpu_custom_call" | custom-call | tf_op jit(solution)/shard_map/pallas_call | solution.py:597
  50.1 0.7 %shard_map.167 = (bf16[1,384]{1,0:T(2,128)(2,1)}, f32[1,384]{1,0:T(1,128)}, f32[64,384]{1,0:T(8,128)}) custom-call(f32[80,384]{1,0:T(8,128)S(1)} %shard_map.166.total), custom_call_target="tpu_custom_call" | custom-call | tf_op jit(solution)/shard_map/pallas_call | solution.py:647
